TPU v7x, 128 devices: a whole 4x4x4 slice. The times are simulated.
128 devices in a mesh: dp: 16 (over z, y_lo, core), fsdp: 8 (over y_hi, x).
Axes of the slice: x: 4, y: 4 (y_hi: 2, y_lo: 2; y = y_hi * 2 + y_lo), z: 4, core: 2. Of those that a mesh axis runs over, the one named last changes fastest.
Arguments:
- queries: bfloat16 [49152, 2048], P(('dp', 'fsdp')), may hold values from -210 to 210
- enc_store: bfloat16 [2048, 128, 512], P(('dp', 'fsdp')), may hold values from -6 to 6
- kv_weight: bfloat16 [512, 2, 2048], P('fsdp'), may hold values from -0.25 to 0.25
- table: int32 [768, 2], replicated, may hold values from 0 to 2047, as said below
- cotangent: bfloat16 [49152, 2048], P(('dp', 'fsdp')), may hold values from -6 to 6
Outputs:
- attended: bfloat16 [49152, 2048], P(('dp', 'fsdp'))
- d_queries: bfloat16 [49152, 2048], P(('dp', 'fsdp'))
- d_store: bfloat16 [2048, 128, 512], P(('dp', 'fsdp'))
- grad_kv: float32 [512, 2, 2048], P('fsdp')
Inputs may be any that keep to these rules, and one draw needn't show every extreme that they name: `table`: the windows of device (d, f) (rows of the arrays in the order dp then fsdp) name only encodings stored on devices (d', f) with the same fsdp index. The 12 encodings named by one device's windows come from exactly 6 encoder devices, 2 from each. An encoding may be named more than once.
All inputs are finite; a program needn't handle non-finite values.
Results may differ from a plain program's by a relative error of at most 0.015.
The roundings to bfloat16 on the way count: a program that leaves them out, or rounds other values in their place, can miss the bound.
Values may be sent and summed in bfloat16 or wider, within the bound.
A program may use at most 192 MiB of HBM per device.

v0:
```python
import jax
import jax.numpy as jnp
from jax import lax
from jax.sharding import PartitionSpec as P

HEAD = 128
WIN = 64
BLOCK = 128
NEIGH = 2
CAP = 2


def attend_windows(query_win, kv_proj, cot_win):
    count = query_win.shape[0]
    heads = kv_proj.shape[3]
    hq_width = heads * HEAD
    scale = HEAD ** (-0.5)
    keys = kv_proj[:, :, 0]
    values = kv_proj[:, :, 1]
    query_heads = query_win.reshape(count, WIN, heads, HEAD)
    cot_heads = cot_win.reshape(count, WIN, heads, HEAD)
    scores = (
        jnp.einsum("gqhd,gkhd->ghqk", query_heads, keys, preferred_element_type=jnp.float32) * scale
    )
    top = jnp.max(scores, axis=-1, keepdims=True)
    expo = jnp.exp(scores - top)
    probs = expo / jnp.sum(expo, axis=-1, keepdims=True)
    probs_b = probs.astype(jnp.bfloat16)
    attended = jnp.einsum(
        "ghqk,gkhd->gqhd", probs_b, values, preferred_element_type=jnp.float32
    ).astype(jnp.bfloat16)
    d_probs = jnp.einsum("gqhd,gkhd->ghqk", cot_heads, values, preferred_element_type=jnp.float32)
    d_values = jnp.einsum("ghqk,gqhd->gkhd", probs_b, cot_heads, preferred_element_type=jnp.float32)
    d_scores = probs * (d_probs - jnp.sum(d_probs * probs, axis=-1, keepdims=True)) * scale
    d_scores = d_scores.astype(jnp.bfloat16)
    d_query = jnp.einsum(
        "ghqk,gkhd->gqhd", d_scores, keys, preferred_element_type=jnp.float32
    ).astype(jnp.bfloat16)
    d_keys = jnp.einsum(
        "ghqk,gqhd->gkhd", d_scores, query_heads, preferred_element_type=jnp.float32
    )
    d_kv = jnp.stack([d_keys, d_values], axis=2).astype(jnp.bfloat16).reshape(-1, 2 * hq_width)
    return (attended.reshape(count * WIN, hq_width), d_query.reshape(count * WIN, hq_width), d_kv)


def shards(queries, enc_store, kv_weight, table, cotangent):
    n_dp = lax.axis_size("dp")
    n_fsdp = lax.axis_size("fsdp")
    my_dp = lax.axis_index("dp")
    my_col = lax.axis_index("fsdp")
    win_dev = queries.shape[0] // WIN
    blk_dev = enc_store.shape[0]
    enc_width = enc_store.shape[2]
    hq_width = kv_weight.shape[2]
    heads = hq_width // HEAD
    n_req = win_dev * NEIGH
    n_slots = n_dp * CAP
    n_rows = n_req * BLOCK
    req_grid = jnp.take(table.reshape(n_dp, n_fsdp, n_req), my_col, axis=1)
    source_dp = req_grid // blk_dev // n_fsdp
    local_blk = req_grid % blk_dev
    req_order = jnp.arange(n_req)
    same_src = source_dp[:, :, None] == source_dp[:, None, :]
    before = req_order[None, None, :] < req_order[None, :, None]
    slot_num = jnp.sum(same_src & before, axis=2)
    slot_ids = jnp.arange(CAP)
    sel_hit = (source_dp[:, None, :] == my_dp) & (slot_num[:, None, :] == slot_ids[None, :, None])
    pick_blk = jnp.sum(jnp.where(sel_hit, local_blk[:, None, :], 0), axis=2)
    filled = jnp.any(sel_hit, axis=2)
    onehot_send = filled[:, :, None] & (pick_blk[:, :, None] == jnp.arange(blk_dev)[None, None, :])
    onehot_send = onehot_send.astype(jnp.bfloat16).reshape(n_slots, blk_dev)
    store_flat = enc_store.reshape(blk_dev, -1)
    outgoing = jnp.dot(onehot_send, store_flat, preferred_element_type=jnp.float32).astype(
        jnp.bfloat16
    )
    outgoing = outgoing.reshape(n_dp, CAP, BLOCK, enc_width)
    incoming = lax.all_to_all(outgoing, "dp", split_axis=0, concat_axis=0, tiled=True)
    my_source = jnp.take(source_dp, my_dp, axis=0)
    my_slot = jnp.take(slot_num, my_dp, axis=0)
    recv_pos = my_source * CAP + my_slot
    onehot_recv = (recv_pos[:, None] == jnp.arange(n_slots)[None, :]).astype(jnp.bfloat16)
    neighbours = jnp.dot(
        onehot_recv, incoming.reshape(n_slots, -1), preferred_element_type=jnp.float32
    )
    enc_rows = neighbours.astype(jnp.bfloat16).reshape(n_rows, enc_width)
    weight_full = lax.all_gather(kv_weight, "fsdp", axis=0, tiled=True).reshape(
        enc_width, 2 * hq_width
    )
    kv_flat = jnp.dot(enc_rows, weight_full, preferred_element_type=jnp.float32)
    kv_proj = kv_flat.astype(jnp.bfloat16).reshape(win_dev, NEIGH * BLOCK, 2, heads, HEAD)
    attended, d_queries, d_kv = attend_windows(
        queries.reshape(win_dev, WIN, hq_width), kv_proj, cotangent.reshape(win_dev, WIN, hq_width)
    )
    d_neigh = lax.dot_general(
        d_kv, weight_full, (((1,), (1,)), ((), ())), preferred_element_type=jnp.float32
    )
    d_neigh = d_neigh.astype(jnp.bfloat16).reshape(n_req, -1)
    going_back = lax.dot_general(
        onehot_recv, d_neigh, (((0,), (0,)), ((), ())), preferred_element_type=jnp.float32
    )
    going_back = going_back.astype(jnp.bfloat16).reshape(n_dp, CAP, BLOCK, enc_width)
    returned = lax.all_to_all(going_back, "dp", split_axis=0, concat_axis=0, tiled=True)
    d_store = lax.dot_general(
        onehot_send,
        returned.reshape(n_slots, -1),
        (((0,), (0,)), ((), ())),
        preferred_element_type=jnp.float32,
    )
    d_store = d_store.astype(jnp.bfloat16).reshape(enc_store.shape)
    grad_scale = float(win_dev * n_dp * n_fsdp * NEIGH * BLOCK) ** (-0.5)
    row_share = lax.psum_scatter(
        lax.dot_general(
            enc_rows, d_kv, (((0,), (0,)), ((), ())), preferred_element_type=jnp.float32
        ),
        "fsdp",
        scatter_dimension=0,
        tiled=True,
    )
    summed = lax.psum(row_share, "dp")
    grad_kv = (summed * grad_scale).reshape(-1, 2, hq_width)
    return (attended, d_queries, d_store, grad_kv)


def solution(mesh):
    in_specs = (
        P(("dp", "fsdp"), None),
        P(("dp", "fsdp"), None, None),
        P("fsdp", None, None),
        P(),
        P(("dp", "fsdp"), None),
    )
    out_specs = (
        P(("dp", "fsdp"), None),
        P(("dp", "fsdp"), None),
        P(("dp", "fsdp"), None, None),
        P("fsdp", None, None),
    )
    return jax.shard_map(shards, mesh=mesh, in_specs=in_specs, out_specs=out_specs, check_vma=False)
```

profile of v0, /device:TPU:1, one launch (start us, length us, event | category | flops | bytes accessed | tf_op | source)
XLA Modules:
  0.0 527.2 jit_solution(667351354800273771)
XLA Ops:
  7.9 2.8 copy.70
  14.1 3.5 copy.71
  17.6 8.1 %all-to-all-start = ((bf16[16,2,128,512]{3,2,1,0:T(8,128)(2,1)}), bf16[16,2,128,512]{3,2,1,0:T(8,128)(2,1)}, u32[]{:S(2)}, u32[]{:S(2)}) async-start(bf16[16,2,128,512]{3,2,1,0:T(8,128)(2,1)} %bitcast.142), calls=%async_computation | async-start | bytes 8388608 | tf_op jit(solution)/shard_map/all_to_all | solution.py:77
  26.0 1.6 copy.77
  29.3 73.3 %all-to-all-done = bf16[16,2,128,512]{3,2,1,0:T(8,128)(2,1)} async-done(((bf16[16,2,128,512]{3,2,1,0:T(8,128)(2,1)}), bf16[16,2,128,512]{3,2,1,0:T(8,128)(2,1)}, u32[]{:S(2)}, u32[]{:S(2)}) %all-to-all-start) | async-done | bytes 4194336 | tf_op jit(solution)/shard_map/all_to_all | solution.py:77
  102.6 4.6 copy.72
  107.9 2.1 reshape.179
  110.5 4.6 copy.73
  115.2 7.0 %fusion.12 = bf16[192,8,32,128]{3,1,2,0:T(8,128)(2,1)S(1)} fusion(bf16[1536,512]{1,0:T(8,128)(2,1)S(1)} %copy-done.5, bf16[512,4096]{1,0:T(8,128)(2,1)S(1)} %bitcast.156), kind=kOutput, calls=%fused_computation.26 | convolution fusion | flops 6448742400 | bytes 18350080 | tf_op jit(solution)/shard_map/dot_general | solution.py:89
  122.1 2.6 copy.74
  124.7 2.4 fusion.59
  127.2 2.3 fusion.8
  129.8 4.5 fusion.60
  135.5 6.3 %fusion.9 = f32[6,16,256,64]{2,3,1,0:T(8,128)} fusion(bf16[6,256,1,16,128]{4,3,2,1,0:T(8,128)(2,1)S(1)} %get-tuple-element.30, bf16[6,64,16,128]{3,2,1,0:T(8,128)(2,1)} %bitcast.151), kind=kOutput, calls=%fused_computation.23 | convolution fusion | flops 402653184 | bytes 14155776 | tf_op jit(solution)/shard_map/gqhd,gkhd->ghqk/dot_general | solution.py:32
  141.8 19.0 %convert_bitcast_fusion = bf16[6,256,1,16,128]{4,1,3,0,2:T(8,128)(2,1)} fusion(bf16[6,64,16,128]{3,2,1,0:T(8,128)(2,1)} %bitcast.152, f32[6,16,64]{2,1,0:T(8,128)S(1)} %get-tuple-element.31, f32[6,16,256,64]{2,3,1,0:T(8,128)} %copy-done.1), kind=kOutput, calls=%fused_computation.19 | convolution fusion | flops 413669632 | bytes 14180352 | tf_op jit(solution)/shard_map/ghqk,gqhd->gkhd/dot_general | solution.py:33
  160.7 43.8 %convert_bitcast_fusion.1 = bf16[6,256,1,16,128]{4,1,3,0,2:T(8,128)(2,1)} fusion(f32[6,16,256,64]{2,3,1,0:T(8,128)} %fusion.9, bf16[6,64,16,128]{3,2,1,0:T(8,128)(2,1)S(1)} %bitcast.150, f32[6,16,64,256]{3,2,1,0:T(8,128)} %get-tuple-element.32, f32[6,16,64]{2,1,0:T(8,128)S(1)} %get-tuple-element.31), kind=kOutput, calls=%fused_computation.20 | convolution fusion | flops 416815360 | bytes 20471808 | tf_op jit(solution)/shard_map/ghqk,gqhd->gkhd/dot_general | solution.py:39
  204.6 6.1 %pad_maximum_fusion = bf16[6,256,2,16,128]{4,1,3,0,2:T(8,128)(2,1)S(1)} fusion(bf16[6,256,1,16,128]{4,1,3,0,2:T(8,128)(2,1)} %convert_bitcast_fusion, bf16[6,256,1,16,128]{4,1,3,0,2:T(8,128)(2,1)} %convert_bitcast_fusion.1), kind=kLoop, calls=%fused_computation.7 | loop fusion | flops 6291456 | bytes 25165824 | tf_op jit(solution)/shard_map/stack | solution.py:42
  210.7 9.6 %copy.66 = bf16[6,256,2,16,128]{4,3,2,1,0:T(8,128)(2,1)} copy(bf16[6,256,2,16,128]{4,1,3,0,2:T(8,128)(2,1)S(1)} %pad_maximum_fusion) | data formatting | bytes 25165824 | tf_op jit(solution)/shard_map/stack | solution.py:42
  220.3 19.4 %convert_element_type.66 = bf16[1536,4096]{1,0:T(8,128)(2,1)} reshape(bf16[6,256,2,16,128]{4,3,2,1,0:T(8,128)(2,1)} %copy.66) | data formatting | bytes 25165824 | tf_op jit(solution)/shard_map/convert_element_type | solution.py:42
  239.8 11.8 %fusion.61 = f32[512,4096]{1,0:T(8,128)} fusion(bf16[1536,512]{1,0:T(8,128)(2,1)S(1)} %copy-done.6, bf16[1536,4096]{1,0:T(8,128)(2,1)} %convert_element_type.66), kind=kOutput, calls=%fused_computation.88 | convolution fusion | flops 6442450944 | bytes 22544384 | tf_op jit(solution)/shard_map/dot_general | solution.py:112
  251.6 11.8 %convolution_convert_fusion.5 = bf16[1536,512]{1,0:T(8,128)(2,1)} fusion(bf16[1536,4096]{1,0:T(8,128)(2,1)} %convert_element_type.66, bf16[512,4096]{1,0:T(8,128)(2,1)} %bitcast.157), kind=kOutput, calls=%fused_computation.29 | convolution fusion | flops 6443237376 | bytes 18350080 | tf_op jit(solution)/shard_map/dot_general | solution.py:94
  263.4 2.2 reshape.184
  266.9 3.4 copy.79
  270.4 5.3 %all-to-all-start.1 = ((bf16[16,2,128,512]{3,2,1,0:T(8,128)(2,1)}), bf16[16,2,128,512]{3,2,1,0:T(8,128)(2,1)}, u32[]{:S(2)}, u32[]{:S(2)}) async-start(bf16[16,2,128,512]{3,2,1,0:T(8,128)(2,1)} %bitcast.141), calls=%async_computation.1 | async-start | bytes 8388608 | tf_op jit(solution)/shard_map/all_to_all | solution.py:102
  275.7 43.4 %fusion.21 = bf16[6,64,16,128]{3,1,2,0:T(8,128)(2,1)S(1)} fusion(bf16[6,256,1,16,128]{4,3,2,1,0:T(8,128)(2,1)} %copy-done.2, f32[6,16,256,64]{2,3,1,0:T(8,128)} %fusion.9, f32[6,16,64,256]{3,2,1,0:T(8,128)} %get-tuple-element.32, f32[6,16,64]{2,1,0:T(8,128)S(1)} %get-tuple-element.31), kind=kOutput, calls=%fused_computation.37 | convolution fusion | flops 414456064 | bytes 20471808 | tf_op jit(solution)/shard_map/ghqk,gkhd->gqhd/dot_general | solution.py:36
  319.1 77.7 %reduce-scatter.2.cloned.1.call-done = f32[64,4096]{1,0:T(8,128)} async-done(((f32[512,4096]{1,0:T(8,128)}), f32[64,4096]{1,0:T(8,128)}) %reduce-scatter.2.cloned.1.call-update) | async-done | bytes 1048592 | tf_op jit(solution)/shard_map/reduce_scatter | solution.py:111
  396.8 15.6 %fusion.22 = bf16[6,64,16,128]{3,1,2,0:T(8,128)(2,1)S(1)} fusion(bf16[6,256,1,16,128]{4,3,2,1,0:T(8,128)(2,1)} %copy-done, f32[6,16,64]{2,1,0:T(8,128)S(1)} %get-tuple-element.31, f32[6,16,256,64]{2,3,1,0:T(8,128)} %copy-done.1), kind=kOutput, calls=%fused_computation.38 | convolution fusion | flops 411310336 | bytes 14180352 | tf_op jit(solution)/shard_map/ghqk,gkhd->gqhd/dot_general | solution.py:29
  414.5 2.7 copy_bitcast_fusion.10
  417.2 4.6 copy.80
  422.6 2.0 copy.81
  424.6 92.7 %all-reduce.2.cloned.1.call-done = f32[64,4096]{1,0:T(8,128)} async-done(((f32[64,4096]{1,0:T(8,128)}), f32[64,4096]{1,0:T(8,128)}) %all-reduce.2.cloned.1.call-update) | async-done | bytes 1048592 | tf_op jit(solution)/shard_map/psum | solution.py:119
  518.6 1.9 reshape.188
  (52 shorter events, 14.5 us)
Async XLA Ops:
  7.2 103.4 %all-gather.2.cloned.1.call-start = ((), (), s32[]{:S(2)}) async-start(), calls=%async_computation.3 | async-start | bytes 4718592 | tf_op jit(solution)/shard_map/all_gather | solution.py:86
  17.6 8.3 %copy-start.7 = (bf16[384,2048]{1,0:T(8,128)(2,1)S(1)}, bf16[384,2048]{1,0:T(8,128)(2,1)}, u32[]{:S(2)}) copy-start(bf16[384,2048]{1,0:T(8,128)(2,1)} %param.11) | copy-start | bytes 4718596
  17.6 9.9 %copy-start.8 = (bf16[384,2048]{1,0:T(8,128)(2,1)S(1)}, bf16[384,2048]{1,0:T(8,128)(2,1)}, u32[]{:S(2)}) copy-start(bf16[384,2048]{1,0:T(8,128)(2,1)} %param.7) | copy-start | bytes 4718596
  17.6 84.9 %all-to-all-start = ((bf16[16,2,128,512]{3,2,1,0:T(8,128)(2,1)}), bf16[16,2,128,512]{3,2,1,0:T(8,128)(2,1)}, u32[]{:S(2)}, u32[]{:S(2)}) async-start(bf16[16,2,128,512]{3,2,1,0:T(8,128)(2,1)} %bitcast.142), calls=%async_computation | async-start | bytes 8388608 | tf_op jit(solution)/shard_map/all_to_all | solution.py:77
  25.7 371.1 %reduce-scatter.2.cloned.1.call-start = ((), (), s32[]{:S(2)}) async-start(), calls=%async_computation.4 | async-start | bytes 9437184 | tf_op jit(solution)/shard_map/reduce_scatter | solution.py:111
  110.0 5.1 copy-start.5
  115.1 7.0 %copy-start.4 = (bf16[64,8,2,2048]{3,1,2,0:T(8,128)(2,1)}, bf16[64,8,2,2048]{3,1,2,0:T(8,128)(2,1)S(1)}, u32[]{:S(2)}) copy-start(bf16[64,8,2,2048]{3,1,2,0:T(8,128)(2,1)S(1)} %copy.73) | copy-start | bytes 12582916
  124.7 2.5 copy-start.3
  127.2 2.7 copy-start.2
  127.2 8.3 %copy-start = (bf16[6,256,1,16,128]{4,3,2,1,0:T(8,128)(2,1)}, bf16[6,256,1,16,128]{4,3,2,1,0:T(8,128)(2,1)S(1)}, u32[]{:S(2)}) copy-start(bf16[6,256,1,16,128]{4,3,2,1,0:T(8,128)(2,1)S(1)} %get-tuple-element.30) | copy-start | bytes 18874372
  129.8 5.2 copy-start.1
  220.3 19.4 %copy-start.6 = (bf16[1536,512]{1,0:T(8,128)(2,1)S(1)}, bf16[1536,512]{1,0:T(8,128)(2,1)}, u32[]{:S(2)}) copy-start(bf16[1536,512]{1,0:T(8,128)(2,1)} %reshape.179) | copy-start | bytes 4718596
  270.4 146.8 %all-to-all-start.1 = ((bf16[16,2,128,512]{3,2,1,0:T(8,128)(2,1)}), bf16[16,2,128,512]{3,2,1,0:T(8,128)(2,1)}, u32[]{:S(2)}, u32[]{:S(2)}) async-start(bf16[16,2,128,512]{3,2,1,0:T(8,128)(2,1)} %bitcast.141), calls=%async_computation.1 | async-start | bytes 8388608 | tf_op jit(solution)/shard_map/all_to_all | solution.py:102
  275.7 241.6 %all-reduce.2.cloned.1.call-start = ((), (), s32[]{:S(2)}) async-start(), calls=%async_computation.5 | async-start | bytes 2097152 | tf_op jit(solution)/shard_map/psum | solution.py:119
Sparse Core Ops, SparseCore 0:
  10.3 100.1 all-gather.1
  251.7 145.0 reduce-scatter.1
  399.3 117.9 all-reduce.1
where the time goes:
time: 532 us; the launch traced here: 527 us
  waiting for transfers between devices  245 us (46%)
  matrix products  165 us (31%)
  local copies, waits for them, and re-layouts  76.6 us (14%)
  between operations  14.2 us (3%)
  starting transfers between devices  13.7 us (3%)
  other arithmetic  12.6 us (2%)
    psum x1, waiting for transfers between devices, shards(): summed = lax.psum(row_share, 'dp')  92.7 us
    reduce_scatter x1, waiting for transfers between devices, shards(): lax.psum_scatter(lax.dot_general(enc_rows, d_kv, (((0,), (0,)), ((), ()))...  77.7 us
    all_to_all x1, waiting for transfers between devices, shards(): lax.all_to_all(outgoing, 'dp', split_axis=0, concat_axis=0, tiled=True)  73.3 us
    dot_general x1, matrix products, attend_windows(): jnp.einsum('ghqk,gqhd->gkhd', d_scores, query_heads, preferred_element_ty...  43.8 us
    dot_general x1, matrix products, attend_windows(): jnp.einsum('ghqk,gkhd->gqhd', d_scores, keys, preferred_element_type=jnp....  43.4 us
    unnamed x29, local copies, waits for them, and re-layouts  33.4 us
    convert_element_type x1, local copies, waits for them, and re-layouts, attend_windows(): jnp.stack([d_keys, d_values], axis=2).astype(jnp.bfloat16)  19.4 us
    dot_general x1, matrix products, attend_windows(): jnp.einsum('ghqk,gqhd->gkhd', probs_b, cot_heads, preferred_element_type=...  19 us
  transfers between devices with their start and end apart: 5, of which 4 were waited for; matrix products, arithmetic and copies ran while one was open for 21% of the time, Pallas kernels for 0%

commit v1 on v0

v1 whole, which is shorter than its diff:
```python
import jax
import jax.numpy as jnp
from jax import lax
from jax.experimental import pallas as pl
from jax.experimental.pallas import tpu as pltpu
from jax.sharding import PartitionSpec as P

HEAD = 128
WIN = 64
BLOCK = 128
NEIGH = 2
CAP = 2
NZ, NY, NC = 4, 2, 2
NYH, NX = 2, 4
N_DP, N_FSDP = NZ * NY * NC, NYH * NX
PHASES = 4
ROWS = BLOCK // PHASES
SCALE = HEAD ** (-0.5)
MESH = pl.DeviceIdType.MESH
f32, bf16 = jnp.float32, jnp.bfloat16
ORDER = (
    (2, 1, 0), (2, 1, 1), (2, 0, 0), (2, 0, 1),
    (1, 1, 0), (3, 1, 0), (1, 1, 1), (3, 1, 1),
    (1, 0, 0), (3, 0, 0), (1, 0, 1), (3, 0, 1),
    (0, 1, 0), (0, 1, 1), (0, 0, 1),
)
GRAD_TILE = 512


def mm(a, b):
    return jnp.dot(a, b, preferred_element_type=f32)


def mm_nt(a, b):
    return lax.dot_general(a, b, (((1,), (1,)), ((), ())), preferred_element_type=f32)


def mm_tn(a, b):
    return lax.dot_general(a, b, (((0,), (0,)), ((), ())), preferred_element_type=f32)


def place():
    dp = lax.axis_index("dp")
    fs = lax.axis_index("fsdp")
    return dp, fs, dp // (NY * NC), (dp // NC) % NY, dp % NC, fs // NX, fs % NX


def two_heads(rows):
    lane = lax.broadcasted_iota(jnp.int32, rows.shape, 1)
    zero = jnp.zeros_like(rows)
    return jnp.concatenate([jnp.where(lane < HEAD, rows, zero), jnp.where(lane < HEAD, zero, rows)], axis=0)


def own_halves(full):
    return jnp.concatenate([full[:WIN, :HEAD], full[WIN:, HEAD:]], axis=1)


def pair_first(loaded):
    query, cot, keys, values = loaded
    query2, cot2 = two_heads(query), two_heads(cot)
    return query2, cot2, mm_nt(keys, query2), mm_nt(values, cot2)


def pair_softmax(first):
    query2, cot2, scores, d_probs = first
    expo = jnp.exp((scores - jnp.max(scores, axis=0, keepdims=True)) * SCALE)
    probs = expo * (1.0 / jnp.sum(expo, axis=0, keepdims=True))
    inner = jnp.sum(d_probs * probs, axis=0, keepdims=True)
    d_scores = ((probs * SCALE) * (d_probs - inner)).astype(bf16)
    return query2, cot2, probs.astype(bf16), d_scores


def pair_last(second, loaded):
    query2, cot2, probs_b, d_scores = second
    _, _, keys, values = loaded
    return (
        own_halves(mm_tn(probs_b, values)).astype(bf16),
        own_halves(mm_tn(d_scores, keys)).astype(bf16),
        mm(d_scores, query2).astype(bf16),
        mm(probs_b, cot2).astype(bf16),
    )


def attend(win, q_ref, c_ref, kv_ref, att_ref, dq_ref):
    width = q_ref.shape[1]
    pairs = width // (2 * HEAD)
    row = pl.ds(pl.multiple_of(win * WIN, WIN), WIN)
    blk = pl.ds(win * NEIGH, NEIGH)
    keys_of = NEIGH * BLOCK

    def cols(pair, base):
        return pl.ds(base + pair * 2 * HEAD, 2 * HEAD)

    loaded = [
        (
            q_ref[row, cols(i, 0)],
            c_ref[row, cols(i, 0)],
            kv_ref[blk, :, cols(i, 0)].reshape(keys_of, 2 * HEAD),
            kv_ref[blk, :, cols(i, width)].reshape(keys_of, 2 * HEAD),
        )
        for i in range(pairs)
    ]
    ahead = 2
    first = [pair_first(loaded[i]) for i in range(min(ahead, pairs))]
    second, last = [], []
    for i in range(pairs):
        second.append(pair_softmax(first[i]))
        if i + ahead < pairs:
            first.append(pair_first(loaded[i + ahead]))
        if i >= 1:
            last.append(pair_last(second[i - 1], loaded[i - 1]))
    last.append(pair_last(second[-1], loaded[-1]))
    for i, (att, d_query, d_key, d_value) in enumerate(last):
        att_ref[row, cols(i, 0)] = att
        dq_ref[row, cols(i, 0)] = d_query
        kv_ref[blk, :, cols(i, 0)] = d_key.reshape(NEIGH, BLOCK, 2 * HEAD)
        kv_ref[blk, :, cols(i, width)] = d_value.reshape(NEIGH, BLOCK, 2 * HEAD)


def first_two(table_ref, base, n_req, source, value_of):
    first, second, count = jnp.int32(0), jnp.int32(0), jnp.int32(0)
    for r in range(n_req):
        entry = table_ref[base + r]
        hit = value_of.source(entry) == source
        value = value_of.value(entry, r)
        first = jnp.where(hit & (count == 0), value, first)
        second = jnp.where(hit & (count == 1), value, second)
        count = count + hit.astype(jnp.int32)
    return first, second, count


class Local:
    def __init__(self, blk_dev):
        self.blk_dev = blk_dev

    def source(self, entry):
        return entry // (self.blk_dev * N_FSDP)

    def value(self, entry, r):
        return entry % self.blk_dev


class Request(Local):
    def value(self, entry, r):
        return jnp.int32(r)


def main_kernel(
    table_ref, q_hbm, store_hbm, w_hbm, c_hbm,
    att_hbm, dq_hbm, back_hbm, grad_hbm,
    q_ref, c_ref, store_ref, w_ref, send_ref, recv0, recv1, recv2, recv3,
    kv_ref, enc_ref, enc_t_ref, att_ref, dq_ref, dn_ref,
    gs_ref, go_ref, gr_ref, rs_ref, ds_ref, dr_ref, ag_ref,
    pick_ref, slot_ref, inv_ref,
    in_sem, out_sem, a_send, a_recv, w_send, w_recv, ws_send, ws_recv,
    b_send, b_recv, g_send, g_recv, r_send, r_recv, d_send, d_recv, o_send, o_recv,
):
    recvs = (recv0, recv1, recv2, recv3)
    dp, fs, z, yl, core, yh, x = place()
    blk_dev = store_ref.shape[0]
    n_req = kv_ref.shape[0]
    hq = q_ref.shape[1]
    enc_width = store_ref.shape[2]
    w_rows = w_hbm.shape[0]
    w_half = w_rows // NC
    sib = (core + 1) % NC

    def dp_dev(dz, dy, dc):
        return (((z + dz) % NZ) * (NY * NC) + ((yl + dy) % NY) * NC + (core + dc) % NC, fs)

    def fs_dev(dyh, dx):
        ylo = (yl + dyh) % NY
        return (z * (NY * NC) + ylo * NC + core, ((yh + dyh) % NYH) * NX + (x + dx) % NX)

    FS = [(dyh, dx) for dyh in range(NYH) for dx in range(NX) if (dyh, dx) != (0, 0)]

    def remote(src, dst, ssem, rsem, dev):
        return pltpu.make_async_remote_copy(
            src_ref=src, dst_ref=dst, send_sem=ssem, recv_sem=rsem, device_id=dev, device_id_type=MESH
        )

    own_w = w_ref.at[fs]
    loads = [
        pltpu.make_async_copy(store_hbm, store_ref, in_sem.at[0]),
        pltpu.make_async_copy(w_hbm.at[pl.ds(0, w_half)], own_w.at[0], in_sem.at[1]),
        pltpu.make_async_copy(w_hbm.at[pl.ds(w_half, w_half)], own_w.at[1], in_sem.at[2]),
        pltpu.make_async_copy(q_hbm, q_ref, in_sem.at[3]),
        pltpu.make_async_copy(c_hbm, c_ref, in_sem.at[4]),
    ]
    for copy in loads:
        copy.start()
    barrier = pltpu.get_barrier_semaphore()
    partners = [dp_dev(*o) for o in ORDER] + [fs_dev(*o) for o in FS]
    for dev in partners:
        pl.semaphore_signal(barrier, inc=1, device_id=dev, device_id_type=MESH)

    def picks(i, carry):
        dst = ((z + i // 4) % NZ) * (NY * NC) + ((yl + (i // 2) % 2) % NY) * NC + (core + i % 2) % NC
        base = (dst * N_FSDP + fs) * n_req
        a, b, _ = first_two(table_ref, base, n_req, dp, Local(blk_dev))
        pick_ref[2 * i] = a
        pick_ref[2 * i + 1] = b
        return carry

    lax.fori_loop(0, N_DP, picks, 0)
    loads[1].wait()
    loads[2].wait()
    loads[0].wait()
    pl.semaphore_wait(barrier, len(partners))

    w_copies = []
    for j, (dyh, dx) in enumerate(FS):
        part = w_ref.at[fs, core]
        copy = remote(part, part, w_send.at[j], w_recv.at[j], fs_dev(dyh, dx))
        copy.start()
        w_copies.append(copy)

    a_copies = []
    for p in range(PHASES):
        rows = pl.ds(p * ROWS, ROWS)
        for dz, dy, dc in ORDER:
            i = dz * 4 + dy * 2 + dc
            for k in range(CAP):
                send_ref[p, 2 * i + k] = store_ref[pick_ref[2 * i + k], rows, :]
            slot = pl.ds(2 * i, CAP)
            copy = remote(send_ref.at[p, slot], recvs[p].at[slot], a_send.at[p, i], a_recv.at[p, i], dp_dev(dz, dy, dc))
            copy.start()
            a_copies.append(copy)
        for k in range(CAP):
            recvs[p][k] = store_ref[pick_ref[k], rows, :]

    mine = (dp * N_FSDP + fs) * n_req

    def slots(i, carry):
        src = ((z + NZ - i // 4) % NZ) * (NY * NC) + ((yl + (i // 2) % 2) % NY) * NC + (core + i % 2) % NC
        a, b, _ = first_two(table_ref, mine, n_req, src, Request(blk_dev))
        inv_ref[2 * i] = a
        inv_ref[2 * i + 1] = b
        return carry

    lax.fori_loop(0, N_DP, slots, 0)
    sources = [table_ref[mine + r] // (blk_dev * N_FSDP) for r in range(n_req)]
    for r in range(n_req):
        s = sources[r]
        dz = (z + NZ - s // (NY * NC)) % NZ
        index = dz * 4 + ((yl + (s // NC) % NY) % NY) * 2 + (core + s % NC) % NC
        seen = jnp.int32(0)
        for earlier in range(r):
            seen = seen + (sources[earlier] == s).astype(jnp.int32)
        slot_ref[r] = index * 2 + jnp.minimum(seen, CAP - 1)

    ws_copies = []
    for j, (dyh, dx) in enumerate(FS):
        w_copies[j].wait_recv()
        src_fs = ((yh + dyh) % NYH) * NX + (x + NX - dx) % NX
        part = w_ref.at[src_fs, core]
        copy = remote(part, part, ws_send.at[j], ws_recv.at[j], dp_dev(0, 0, 1))
        copy.start()
        ws_copies.append(copy)
    for copy in ws_copies:
        copy.wait_recv()

    for p in range(PHASES):
        for copy in a_copies[p * len(ORDER):(p + 1) * len(ORDER)]:
            copy.wait_recv()
        rows = pl.ds(p * ROWS, ROWS)
        for r in range(n_req):
            enc_ref[p, r] = recvs[p][slot_ref[r]]

        @pl.loop(0, kv_ref.shape[2] // 1024)
        def _(t):
            c = pl.ds(pl.multiple_of(t * 1024, 1024), 1024)
            out = mm(enc_ref[p].reshape(n_req * ROWS, enc_width), w_ref[:, :, :, c].reshape(enc_width, 1024))
            kv_ref[:, rows, c] = out.astype(bf16).reshape(n_req, ROWS, 1024)

    loads[3].wait()
    loads[4].wait()

    @pl.loop(0, n_req // NEIGH)
    def _(win):
        attend(win, q_ref, c_ref, kv_ref, att_ref, dq_ref)

    outs = [
        pltpu.make_async_copy(att_ref, att_hbm, out_sem.at[0]),
        pltpu.make_async_copy(dq_ref, dq_hbm, out_sem.at[1]),
    ]
    for copy in outs:
        copy.start()
    for copy in a_copies:
        copy.wait_send()

    b_copies = []
    for p in range(PHASES):
        rows = pl.ds(p * ROWS, ROWS)
        lhs = kv_ref[:, rows, :].reshape(n_req * ROWS, 2 * hq)

        @pl.loop(0, 2)
        def _(t):
            part = w_ref[pl.ds(t * (N_FSDP // 2), N_FSDP // 2)].reshape(enc_width // 2, 2 * hq)
            c = pl.ds(pl.multiple_of(t * (enc_width // 2), enc_width // 2), enc_width // 2)
            dn_ref[:, :, c] = mm_nt(lhs, part).astype(bf16).reshape(n_req, ROWS, enc_width // 2)

        for dz, dy, dc in ORDER + ((0, 0, 0),):
            i = dz * 4 + dy * 2 + dc
            for k in range(CAP):
                send_ref[p, 2 * i + k] = dn_ref[inv_ref[2 * i + k]]
            slot = pl.ds(2 * i, CAP)
            if i == 0:
                copy = pltpu.make_async_copy(send_ref.at[p, slot], back_hbm.at[p, slot], out_sem.at[2 + p])
                outs.append(copy)
            else:
                copy = remote(
                    send_ref.at[p, slot], back_hbm.at[p, slot], b_send.at[p, i], b_recv.at[p, i],
                    dp_dev((NZ - dz) % NZ, dy, dc),
                )
                b_copies.append(copy)
            copy.start()

    enc_rows = jnp.concatenate([enc_ref[p] for p in range(PHASES)], axis=1).reshape(n_req * BLOCK, enc_width)
    enc_t_ref[...] = enc_rows.T

    def grad_tile(half, t):
        c = pl.ds(pl.multiple_of(half * hq + t * GRAD_TILE, GRAD_TILE), GRAD_TILE)
        return mm(enc_t_ref[...], kv_ref[:, :, c].reshape(n_req * BLOCK, GRAD_TILE)).reshape(
            N_FSDP, w_rows, GRAD_TILE
        )

    n_tiles = hq // GRAD_TILE
    g_copies = []
    for t in range(n_tiles):
        gs_ref[t] = grad_tile(sib, t).astype(bf16)
        copy = remote(gs_ref.at[t], gr_ref.at[t], g_send.at[t], g_recv.at[t], dp_dev(0, 0, 1))
        copy.start()
        g_copies.append(copy)
    for t in range(n_tiles):
        go_ref[t] = grad_tile(core, t)
    r_copies = []
    for t in range(n_tiles):
        g_copies[t].wait()
        both = go_ref[t] + gr_ref[t].astype(f32)
        gs_ref[t] = both.astype(bf16)
        for j, (dyh, dx) in enumerate(FS):
            dst_fs = ((yh + dyh) % NYH) * NX + (x + dx) % NX
            copy = remote(gs_ref.at[t, dst_fs], rs_ref.at[t, j], r_send.at[t, j], r_recv.at[t, j], fs_dev(dyh, dx))
            copy.start()
            r_copies.append(copy)
    part_cols = hq // (NZ * NY)
    per_tile = GRAD_TILE // part_cols
    for t in range(n_tiles):
        for copy in r_copies[t * len(FS):(t + 1) * len(FS)]:
            copy.wait_recv()
        total = gs_ref[t, fs].astype(f32)
        for j in range(len(FS)):
            total = total + rs_ref[t, j].astype(f32)
        for s in range(per_tile):
            ds_ref[t * per_tile + s] = total[:, s * part_cols:(s + 1) * part_cols].astype(bf16)
    chips = [(dz, dy) for dz in range(NZ) for dy in range(NY) if (dz, dy) != (0, 0)]
    d_copies = []
    for m, (dz, dy) in enumerate(chips):
        chip = ((z + dz) % NZ) * NY + (yl + dy) % NY
        copy = remote(ds_ref.at[chip], dr_ref.at[m], d_send.at[m], d_recv.at[m], dp_dev(dz, dy, 0))
        copy.start()
        d_copies.append(copy)
    own_chip = z * NY + yl
    total = ds_ref[own_chip].astype(f32)
    for m in range(len(chips)):
        d_copies[m].wait_recv()
        total = total + dr_ref[m].astype(f32)
    ag_ref[...] = total.astype(bf16)
    piece = grad_hbm.at[core * (NZ * NY) + own_chip]
    copy = pltpu.make_async_copy(ag_ref, piece, out_sem.at[2 + PHASES])
    copy.start()
    outs.append(copy)
    o_copies = []
    for dz, dy, dc in ORDER:
        i = dz * 4 + dy * 2 + dc
        copy = remote(ag_ref, piece, o_send.at[i], o_recv.at[i], dp_dev(dz, dy, dc))
        copy.start()
        o_copies.append(copy)
    for copy in outs:
        copy.wait()
    for copy in w_copies + ws_copies + r_copies + d_copies:
        copy.wait_send()
    for copy in b_copies + o_copies:
        copy.wait()


def main_call(table, queries, enc_store, weight, cotangent):
    tokens, hq = queries.shape
    blk_dev, _, enc_width = enc_store.shape
    n_req = tokens // WIN * NEIGH
    w_rows = weight.shape[0]
    n_slots = N_DP * CAP
    n_tiles = hq // GRAD_TILE
    n_chips = NZ * NY
    hbm = pl.BlockSpec(memory_space=pl.ANY)
    vm = pltpu.VMEM
    sem = pltpu.SemaphoreType.DMA
    recv = vm((n_slots, ROWS, enc_width), bf16)
    scratch = [
        vm((tokens, hq), bf16), vm((tokens, hq), bf16), vm(enc_store.shape, bf16),
        vm((N_FSDP, NC, w_rows // NC, 2 * hq), bf16), vm((PHASES, n_slots, ROWS, enc_width), bf16),
        recv, recv, recv, recv,
        vm((n_req, BLOCK, 2 * hq), bf16), vm((PHASES, n_req, ROWS, enc_width), bf16),
        vm((enc_width, n_req * BLOCK), bf16), vm((tokens, hq), bf16), vm((tokens, hq), bf16),
        vm((n_req, ROWS, enc_width), bf16),
        vm((n_tiles, N_FSDP, w_rows, GRAD_TILE), bf16), vm((n_tiles, N_FSDP, w_rows, GRAD_TILE), f32),
        vm((n_tiles, N_FSDP, w_rows, GRAD_TILE), bf16), vm((n_tiles, N_FSDP - 1, w_rows, GRAD_TILE), bf16),
        vm((n_chips, w_rows, hq // n_chips), bf16), vm((n_chips - 1, w_rows, hq // n_chips), bf16),
        vm((w_rows, hq // n_chips), bf16),
        pltpu.SMEM((n_slots,), jnp.int32), pltpu.SMEM((n_req,), jnp.int32), pltpu.SMEM((n_slots,), jnp.int32),
        sem((5,)), sem((3 + PHASES,)), sem((PHASES, N_DP)), sem((PHASES, N_DP)),
        sem((N_FSDP - 1,)), sem((N_FSDP - 1,)), sem((N_FSDP - 1,)), sem((N_FSDP - 1,)),
        sem((PHASES, N_DP)), sem((PHASES, N_DP)), sem((n_tiles,)), sem((n_tiles,)),
        sem((n_tiles, N_FSDP - 1)), sem((n_tiles, N_FSDP - 1)), sem((n_chips - 1,)), sem((n_chips - 1,)),
        sem((N_DP,)), sem((N_DP,)),
    ]
    return pl.pallas_call(
        main_kernel,
        out_shape=[
            jax.ShapeDtypeStruct((tokens, hq), bf16),
            jax.ShapeDtypeStruct((tokens, hq), bf16),
            jax.ShapeDtypeStruct((PHASES, n_slots, ROWS, enc_width), bf16),
            jax.ShapeDtypeStruct((NC * n_chips, w_rows, hq // n_chips), bf16),
        ],
        in_specs=[pl.BlockSpec(memory_space=pltpu.SMEM), hbm, hbm, hbm, hbm],
        out_specs=[hbm, hbm, hbm, hbm],
        scratch_shapes=scratch,
        compiler_params=pltpu.CompilerParams(collective_id=0, has_side_effects=True, vmem_limit_bytes=62 << 20),
        name="attend_exchange",
    )(table, queries, enc_store, weight, cotangent)


def last_kernel(table_ref, back_ref, g_ref, store_ref, grad_ref, acc_ref):
    dp, fs, z, yl, core, _, _ = place()
    blk_dev = store_ref.shape[0]
    n_req = table_ref.shape[0] // (N_DP * N_FSDP)
    acc_ref[...] = jnp.zeros_like(acc_ref)

    def add(i, carry):
        dst = ((z + i // 4) % NZ) * (NY * NC) + ((yl + (i // 2) % 2) % NY) * NC + (core + i % 2) % NC
        base = (dst * N_FSDP + fs) * n_req
        a, b, count = first_two(table_ref, base, n_req, dp, Local(blk_dev))

        @pl.when(count > 0)
        def _():
            acc_ref[a] = acc_ref[a] + back_ref[0, 2 * i].astype(f32)

        @pl.when(count > 1)
        def _():
            acc_ref[b] = acc_ref[b] + back_ref[0, 2 * i + 1].astype(f32)

        return carry

    lax.fori_loop(0, N_DP, add, 0)
    store_ref[...] = acc_ref[...].astype(bf16)

    @pl.when(pl.program_id(0) == 0)
    def _():
        scale = float(n_req * N_DP * N_FSDP * BLOCK) ** (-0.5)
        cols = g_ref.shape[2]
        for half in range(NC):
            for chip in range(NZ * NY):
                grad_ref[:, half, chip * cols:(chip + 1) * cols] = g_ref[half * NZ * NY + chip].astype(f32) * scale


def last_call(table, back, grads, store_shape, w_rows, hq):
    blk_dev, _, enc_width = store_shape
    return pl.pallas_call(
        last_kernel,
        grid=(PHASES,),
        out_shape=[
            jax.ShapeDtypeStruct(store_shape, bf16),
            jax.ShapeDtypeStruct((w_rows, NC, hq), f32),
        ],
        in_specs=[
            pl.BlockSpec(memory_space=pltpu.SMEM),
            pl.BlockSpec((1,) + back.shape[1:], lambda p: (p, 0, 0, 0)),
            pl.BlockSpec(grads.shape, lambda p: (0, 0, 0)),
        ],
        out_specs=[
            pl.BlockSpec((blk_dev, ROWS, enc_width), lambda p: (0, p, 0)),
            pl.BlockSpec((w_rows, NC, hq), lambda p: (0, 0, 0)),
        ],
        scratch_shapes=[pltpu.VMEM((blk_dev, ROWS, enc_width), f32)],
        compiler_params=pltpu.CompilerParams(vmem_limit_bytes=40 << 20),
        name="store_gradient",
    )(table, back, grads)


def shards(queries, enc_store, kv_weight, table, cotangent):
    w_rows, _, hq = kv_weight.shape
    table = table.reshape(-1)
    attended, d_queries, back, grads = main_call(
        table, queries, enc_store, kv_weight.reshape(w_rows, 2 * hq), cotangent
    )
    d_store, grad_kv = last_call(table, back, grads, enc_store.shape, w_rows, hq)
    return attended, d_queries, d_store, grad_kv


def solution(mesh):
    in_specs = (
        P(("dp", "fsdp"), None),
        P(("dp", "fsdp"), None, None),
        P("fsdp", None, None),
        P(),
        P(("dp", "fsdp"), None),
    )
    out_specs = (
        P(("dp", "fsdp"), None),
        P(("dp", "fsdp"), None),
        P(("dp", "fsdp"), None, None),
        P("fsdp", None, None),
    )
    return jax.shard_map(shards, mesh=mesh, in_specs=in_specs, out_specs=out_specs, check_vma=False)
```

time: 532 us -> 157 us (0.30)
  waiting for transfers between devices: 245 us -> 0 us
  matrix products: 165 us -> 0 us
  Pallas kernels: 0 us -> 146 us
  local copies, waits for them, and re-layouts: 76.6 us -> 10 us
  starting transfers between devices: 13.7 us -> 0 us
  between operations: 14.2 us -> 0.67 us
  other arithmetic: 12.6 us -> 0 us
    dot_general x13 -> x0, matrix products: 165 us -> none  [the longest x1 43.8 us: attend_windows(): jnp.einsum('ghqk,gqhd->gkhd', d_scores, query_heads, preferred_element_ty...]
    pallas_call x0 -> x2, Pallas kernels: none -> 146 us  [the longest x1 134 us: main_call(): pl.pallas_call(main_kernel, out_shape=[jax.ShapeDtypeStruct((tokens, hq),...]
    psum x1 -> x0, waiting for transfers between devices: 92.7 us -> none  [shards(): summed = lax.psum(row_share, 'dp')]
    reduce_scatter x1 -> x0, waiting for transfers between devices: 77.7 us -> none  [shards(): lax.psum_scatter(lax.dot_general(enc_rows, d_kv, (((0,), (0,)), ((), ()))...]
    all_to_all x2 -> x0, waiting for transfers between devices: 73.3 us -> none  [the longest x1 73.3 us: shards(): lax.all_to_all(outgoing, 'dp', split_axis=0, concat_axis=0, tiled=True)]
    unnamed x29 -> x14, local copies, waits for them, and re-layouts: 33.4 us -> 9.21 us
    convert_element_type x3 -> x0, local copies, waits for them, and re-layouts: 21.5 us -> none  [the longest x1 19.4 us: attend_windows(): jnp.stack([d_keys, d_values], axis=2).astype(jnp.bfloat16)]
    all_to_all x2 -> x0, starting transfers between devices: 13.4 us -> none  [the longest x1 8.11 us: shards(): lax.all_to_all(outgoing, 'dp', split_axis=0, concat_axis=0, tiled=True)]
  transfers between devices with their start and end apart: 5 -> 0, of which waited for: 4 -> 0; matrix products, arithmetic and copies ran while one was open for 21% -> 0% of each run, Pallas kernels for 0% -> 0%
where the time goes in v1:
time: 157 us
  Pallas kernels  146 us (93%)
  local copies, waits for them, and re-layouts  10 us (6%)
    pallas_call x1, Pallas kernels, main_call(): pl.pallas_call(main_kernel, out_shape=[jax.ShapeDtypeStruct((tokens, hq),...  134 us
    pallas_call x1, Pallas kernels, last_call(): pl.pallas_call(last_kernel, grid=(PHASES,), out_shape=[jax.ShapeDtypeStru...  12.7 us
    unnamed x14, local copies, waits for them, and re-layouts  9.21 us

profile of v1, /device:TPU:1, one launch (start us, length us, event | category | flops | bytes accessed | tf_op | source)
XLA Modules:
  0.0 157.0 jit_solution(3255092610412428902)
XLA Ops:
  0.6 0.9 copy.9
  1.5 0.8 reshape.14.table_ref
  2.3 2.0 %copy.10 = bf16[8,8,2,2048]{3,1,2,0:T(8,128)(2,1)} copy(bf16[8,8,2,2048]{3,2,1,0:T(2,128)(2,1)} %bitcast.3) | data formatting | bytes 1048576
  4.3 0.0 copy-start.2
  4.3 133.6 %attend_exchange.1 = (bf16[384,2048]{1,0:T(8,128)(2,1)}, bf16[384,2048]{1,0:T(8,128)(2,1)}, bf16[4,32,32,512]{3,2,1,0:T(8,128)(2,1)}, bf16[16,64,256]{2,1,0:T(8,128)(2,1)}) custom-call(s32[1536]{0:T(1024)} %reshape.14.table_ref, bf16[384,2048]{1,0:T(8,128)(2,1)} %q_hbm.1, bf16[16,128,512]{2,1,0:T(8,128)(2,1)} %store_hbm.1, bf16[64,4096]{1,0:T(8,128)(2,1)} %bitcast.2, ...), custom_call_target="tpu_custom_call" | custom-call | tf_op jit(solution)/shard_map/attend_exchange/pallas_call | solution.py:418
  137.9 0.0 copy-done.2
  137.9 0.0 copy-start
  137.9 2.2 %copy-done = bf16[4,32,32,512]{3,2,1,0:T(8,128)(2,1)S(1)} copy-done((bf16[4,32,32,512]{3,2,1,0:T(8,128)(2,1)S(1)}, bf16[4,32,32,512]{3,2,1,0:T(8,128)(2,1)}, u32[]{:S(2)}) %copy-start) | copy-done | bytes 4194328
  140.1 0.0 copy-start.1
  140.1 1.0 copy-done.1
  141.2 0.0 copy-start.4
  141.2 12.7 %store_gradient.1 = (bf16[16,128,512]{2,1,0:T(8,128)(2,1)}, f32[64,2,2048]{2,1,0:T(2,128)}) custom-call(s32[1536]{0:T(1024)S(1)} %copy-done.2, bf16[4,32,32,512]{3,2,1,0:T(8,128)(2,1)S(1)} %copy-done, bf16[16,64,256]{2,1,0:T(8,128)(2,1)S(1)} %copy-done.1), custom_call_target="tpu_custom_call" | custom-call | tf_op jit(solution)/shard_map/store_gradient/pallas_call | solution.py:469
  153.8 0.0 copy-done.4
  153.9 0.0 copy-start.3
  153.9 1.1 copy.13
  155.0 0.8 copy-done.3
  155.8 1.1 copy.14
Async XLA Ops:
  4.3 133.6 %copy-start.2 = (s32[1536]{0:T(1024)S(1)}, s32[1536]{0:T(1024)}, u32[]{:S(2)}) copy-start(s32[1536]{0:T(1024)} %reshape.14.table_ref) | copy-start | bytes 18436
  137.9 2.2 %copy-start = (bf16[4,32,32,512]{3,2,1,0:T(8,128)(2,1)S(1)}, bf16[4,32,32,512]{3,2,1,0:T(8,128)(2,1)}, u32[]{:S(2)}) copy-start(bf16[4,32,32,512]{3,2,1,0:T(8,128)(2,1)} %get-tuple-element.12.back_ref) | copy-start | bytes 12582916
  140.1 1.0 copy-start.1
  141.2 12.7 %copy-start.4 = (bf16[384,2048]{1,0:T(8,128)(2,1)S(1)}, bf16[384,2048]{1,0:T(8,128)(2,1)}, u32[]{:S(2)}) copy-start(bf16[384,2048]{1,0:T(8,128)(2,1)} %get-tuple-element.20) | copy-start | bytes 4718596
  153.9 2.0 %copy-start.3 = (bf16[384,2048]{1,0:T(8,128)(2,1)S(1)}, bf16[384,2048]{1,0:T(8,128)(2,1)}, u32[]{:S(2)}) copy-start(bf16[384,2048]{1,0:T(8,128)(2,1)} %get-tuple-element.21) | copy-start | bytes 4718596

commit v2 on v1

v2 whole, which is shorter than its diff:
```python
import functools

import jax
import jax.numpy as jnp
from jax import lax
from jax.experimental import pallas as pl
from jax.experimental.pallas import tpu as pltpu
from jax.sharding import PartitionSpec as P

HEAD = 128
WIN = 64
BLOCK = 128
NEIGH = 2
CAP = 2
NZ, NY, NC = 4, 2, 2
NYH, NX = 2, 4
N_DP, N_FSDP = NZ * NY * NC, NYH * NX
PHASES = 4
ROWS = BLOCK // PHASES
SCALE = HEAD ** (-0.5)
MESH = pl.DeviceIdType.MESH
f32, bf16 = jnp.float32, jnp.bfloat16
ORDER = (
    (2, 1, 0), (2, 1, 1), (2, 0, 0), (2, 0, 1),
    (1, 1, 0), (3, 1, 0), (1, 1, 1), (3, 1, 1),
    (1, 0, 0), (3, 0, 0), (1, 0, 1), (3, 0, 1),
    (0, 1, 0), (0, 1, 1), (0, 0, 1),
)
STEPS = (2, 1, 3, 0)


def mm(a, b):
    return jnp.dot(a, b, preferred_element_type=f32)


def mm_nt(a, b):
    return lax.dot_general(a, b, (((1,), (1,)), ((), ())), preferred_element_type=f32)


def mm_tn(a, b):
    return lax.dot_general(a, b, (((0,), (0,)), ((), ())), preferred_element_type=f32)


def place():
    dp = lax.axis_index("dp")
    fs = lax.axis_index("fsdp")
    return dp, fs, dp // (NY * NC), (dp // NC) % NY, dp % NC, fs // NX, fs % NX


def two_heads(rows):
    lane = lax.broadcasted_iota(jnp.int32, rows.shape, 1)
    zero = jnp.zeros_like(rows)
    return jnp.concatenate([jnp.where(lane < HEAD, rows, zero), jnp.where(lane < HEAD, zero, rows)], axis=0)


def own_halves(full):
    return jnp.concatenate([full[:WIN, :HEAD], full[WIN:, HEAD:]], axis=1)


def pair_first(loaded):
    query, cot, keys, values = loaded
    query2, cot2 = two_heads(query), two_heads(cot)
    return query2, cot2, mm_nt(keys, query2), mm_nt(values, cot2)


def pair_softmax(first):
    query2, cot2, scores, d_probs = first
    expo = jnp.exp((scores - jnp.max(scores, axis=0, keepdims=True)) * SCALE)
    probs = expo * (1.0 / jnp.sum(expo, axis=0, keepdims=True))
    inner = jnp.sum(d_probs * probs, axis=0, keepdims=True)
    d_scores = ((probs * SCALE) * (d_probs - inner)).astype(bf16)
    return query2, cot2, probs.astype(bf16), d_scores


def pair_last(second):
    query2, cot2, probs_b, d_scores = second
    return probs_b, d_scores, mm(d_scores, query2).astype(bf16), mm(probs_b, cot2).astype(bf16)


def window_slices(win, width):
    row = pl.ds(pl.multiple_of(win * WIN, WIN), WIN)
    blk = pl.ds(win * NEIGH, NEIGH)

    def cols(pair, base):
        return pl.ds(base + pair * 2 * HEAD, 2 * HEAD)

    return row, blk, cols, width // (2 * HEAD)


def attend(win, q_ref, c_ref, kv_ref, dkv_ref, probs_ref, ds_ref):
    width = q_ref.shape[1]
    row, blk, cols, pairs = window_slices(win, width)
    keys_of = NEIGH * BLOCK
    loaded = [
        (
            q_ref[row, cols(i, 0)],
            c_ref[row, cols(i, 0)],
            kv_ref[blk, :, cols(i, 0)].reshape(keys_of, 2 * HEAD),
            kv_ref[blk, :, cols(i, width)].reshape(keys_of, 2 * HEAD),
        )
        for i in range(pairs)
    ]
    ahead = 2
    first = [pair_first(loaded[i]) for i in range(min(ahead, pairs))]
    second, last = [], []
    for i in range(pairs):
        second.append(pair_softmax(first[i]))
        if i + ahead < pairs:
            first.append(pair_first(loaded[i + ahead]))
        if i >= 1:
            last.append(pair_last(second[i - 1]))
    last.append(pair_last(second[-1]))
    for i, (probs_b, d_scores, d_key, d_value) in enumerate(last):
        probs_ref[win, i] = probs_b
        ds_ref[win, i] = d_scores
        dkv_ref[blk, :, cols(i, 0)] = d_key.reshape(NEIGH, BLOCK, 2 * HEAD)
        dkv_ref[blk, :, cols(i, width)] = d_value.reshape(NEIGH, BLOCK, 2 * HEAD)


def attend_outputs(win, kv_ref, probs_ref, ds_ref, att_ref, dq_ref):
    width = att_ref.shape[1]
    row, blk, cols, pairs = window_slices(win, width)
    keys_of = NEIGH * BLOCK
    outs = []
    for i in range(pairs):
        keys = kv_ref[blk, :, cols(i, 0)].reshape(keys_of, 2 * HEAD)
        values = kv_ref[blk, :, cols(i, width)].reshape(keys_of, 2 * HEAD)
        outs.append((own_halves(mm_tn(probs_ref[win, i], values)), own_halves(mm_tn(ds_ref[win, i], keys))))
    for i, (att, d_query) in enumerate(outs):
        att_ref[row, cols(i, 0)] = att.astype(bf16)
        dq_ref[row, cols(i, 0)] = d_query.astype(bf16)


def first_two(table_ref, device, n_req, source, blk_dev, by_request):
    first, second = jnp.int32(-1), jnp.int32(-1)
    owned = blk_dev * N_FSDP
    for r in reversed(range(n_req)):
        entry = table_ref[r % NEIGH, device * (n_req // NEIGH) + r // NEIGH]
        hit = lax.div(entry, owned) == source
        value = jnp.int32(r) if by_request else lax.rem(entry, blk_dev)
        second = jnp.where(hit, first, second)
        first = jnp.where(hit, value, first)
    return first, second


def main_kernel(
    table_ref, q_hbm, store_hbm, w_hbm, c_hbm,
    att_hbm, dq_hbm, back_hbm, grad_hbm, pick_ref,
    q_ref, c_ref, store_ref, w_raw, w_ref, send_ref, recv0, recv1, recv2, recv3,
    kv_ref, dkv_ref, probs_ref, dsc_ref, enc_ref, enc_t_ref, dn_ref,
    gs_ref, gr_ref, rs_ref, ds_ref, dr_ref, ag_ref,
    slot_ref, inv_ref,
    in_sem, out_sem, a_send, a_recv, w_send, w_recv, ws_send, ws_recv,
    b_send, b_recv, g_send, g_recv, r_send, r_recv, d_send, d_recv, o_send, o_recv, s_send, s_recv,
):
    recvs = (recv0, recv1, recv2, recv3)
    dp, fs, z, yl, core, yh, x = place()
    blk_dev = store_ref.shape[0]
    n_req = kv_ref.shape[0]
    hq = q_ref.shape[1]
    enc_width = store_ref.shape[2]
    w_rows = w_hbm.shape[0]
    w_half = w_rows // NC
    grad_cols = hq // NZ
    sib = (core + 1) % NC

    def dp_dev(dz, dy, dc):
        return (((z + dz) % NZ) * (NY * NC) + ((yl + dy) % NY) * NC + (core + dc) % NC, fs)

    def fs_dev(dyh, dx):
        ylo = (yl + dyh) % NY
        return (z * (NY * NC) + ylo * NC + core, ((yh + dyh) % NYH) * NX + (x + dx) % NX)

    FS = [(dyh, dx) for dyh in range(NYH) for dx in range(NX) if (dyh, dx) != (0, 0)]

    def remote(src, dst, ssem, rsem, dev):
        return pltpu.make_async_remote_copy(
            src_ref=src, dst_ref=dst, send_sem=ssem, recv_sem=rsem, device_id=dev, device_id_type=MESH
        )

    loads = [
        pltpu.make_async_copy(store_hbm, store_ref, in_sem.at[0]),
        pltpu.make_async_copy(w_hbm, w_raw, in_sem.at[1]),
        pltpu.make_async_copy(q_hbm, q_ref, in_sem.at[2]),
        pltpu.make_async_copy(c_hbm, c_ref, in_sem.at[3]),
    ]
    for copy in loads:
        copy.start()
    barrier = pltpu.get_barrier_semaphore()
    partners = [dp_dev(*o) for o in ORDER] + [fs_dev(*o) for o in FS]
    for dev in partners:
        pl.semaphore_signal(barrier, inc=1, device_id=dev, device_id_type=MESH)

    def picks(i, carry):
        dst = ((z + i // 4) % NZ) * (NY * NC) + ((yl + (i // 2) % 2) % NY) * NC + (core + i % 2) % NC
        a, b = first_two(table_ref, dst * N_FSDP + fs, n_req, dp, blk_dev, False)
        pick_ref[2 * i] = a
        pick_ref[2 * i + 1] = b
        return carry

    lax.fori_loop(0, N_DP, picks, 0)
    loads[0].wait()
    pl.semaphore_wait(barrier, len(partners))

    a_copies, w_copies = [], []
    for p in range(PHASES):
        rows = pl.ds(p * ROWS, ROWS)
        for dz, dy, dc in ORDER:
            i = dz * 4 + dy * 2 + dc
            for k in range(CAP):
                send_ref[p, 2 * i + k] = store_ref[jnp.maximum(pick_ref[2 * i + k], 0), rows, :]
            slot = pl.ds(2 * i, CAP)
            copy = remote(send_ref.at[p, slot], recvs[p].at[slot], a_send.at[p, i], a_recv.at[p, i], dp_dev(dz, dy, dc))
            copy.start()
            a_copies.append(copy)
        for k in range(CAP):
            recvs[p][k] = store_ref[jnp.maximum(pick_ref[k], 0), rows, :]
        if p == 0:
            loads[1].wait()
            for part in range(NC):
                for kind in range(2):
                    w_ref[fs, part, :, kind * hq:(kind + 1) * hq] = w_raw[part * w_half:(part + 1) * w_half, kind, :]
            for j, (dyh, dx) in enumerate(FS):
                part = w_ref.at[fs, core]
                copy = remote(part, part, w_send.at[j], w_recv.at[j], fs_dev(dyh, dx))
                copy.start()
                w_copies.append(copy)

    mine = dp * N_FSDP + fs

    def slots(i, carry):
        src = ((z + NZ - i // 4) % NZ) * (NY * NC) + ((yl + (i // 2) % 2) % NY) * NC + (core + i % 2) % NC
        a, b = first_two(table_ref, mine, n_req, src, blk_dev, True)
        inv_ref[2 * i] = jnp.maximum(a, 0)
        inv_ref[2 * i + 1] = jnp.maximum(b, 0)
        return carry

    lax.fori_loop(0, N_DP, slots, 0)
    sources = [
        lax.div(table_ref[r % NEIGH, mine * (n_req // NEIGH) + r // NEIGH], blk_dev * N_FSDP) for r in range(n_req)
    ]
    for r in range(n_req):
        s = sources[r]
        dz = lax.rem(z + NZ - lax.div(s, NY * NC), NZ)
        dy = lax.rem(yl + lax.rem(lax.div(s, NC), NY), NY)
        index = dz * 4 + dy * 2 + lax.rem(core + lax.rem(s, NC), NC)
        seen = jnp.int32(0)
        for earlier in range(r):
            seen = seen + (sources[earlier] == s).astype(jnp.int32)
        slot_ref[r] = index * 2 + jnp.minimum(seen, CAP - 1)

    ws_copies = []
    for j, (dyh, dx) in enumerate(FS):
        w_copies[j].wait_recv()
        src_fs = ((yh + dyh) % NYH) * NX + (x + NX - dx) % NX
        part = w_ref.at[src_fs, core]
        copy = remote(part, part, ws_send.at[j], ws_recv.at[j], dp_dev(0, 0, 1))
        copy.start()
        ws_copies.append(copy)
    for copy in ws_copies:
        copy.wait_recv()

    for p in range(PHASES):
        for copy in a_copies[p * len(ORDER):(p + 1) * len(ORDER)]:
            copy.wait_recv()
        rows = pl.ds(p * ROWS, ROWS)
        for r in range(n_req):
            enc_ref[p, r] = recvs[p][slot_ref[r]]

        @pl.loop(0, kv_ref.shape[2] // 1024)
        def _(t):
            c = pl.ds(pl.multiple_of(t * 1024, 1024), 1024)
            out = mm(enc_ref[p].reshape(n_req * ROWS, enc_width), w_ref[:, :, :, c].reshape(enc_width, 1024))
            kv_ref[:, rows, c] = out.astype(bf16).reshape(n_req, ROWS, 1024)

    loads[2].wait()
    loads[3].wait()

    @pl.loop(0, n_req // NEIGH)
    def _(win):
        attend(win, q_ref, c_ref, kv_ref, dkv_ref, probs_ref, dsc_ref)

    outs = []
    for copy in a_copies:
        copy.wait_send()

    b_copies = []

    def d_neigh(p):
        rows = pl.ds(p * ROWS, ROWS)
        lhs = dkv_ref[:, rows, :].reshape(n_req * ROWS, 2 * hq)

        @pl.loop(0, 2)
        def _(t):
            part = w_ref[pl.ds(t * (N_FSDP // 2), N_FSDP // 2)].reshape(enc_width // 2, 2 * hq)
            c = pl.ds(pl.multiple_of(t * (enc_width // 2), enc_width // 2), enc_width // 2)
            dn_ref[:, :, c] = mm_nt(lhs, part).astype(bf16).reshape(n_req, ROWS, enc_width // 2)

        for i in range(N_DP):
            for k in range(CAP):
                send_ref[p, 2 * i + k] = dn_ref[inv_ref[2 * i + k]]
        slot = pl.ds(0, CAP)
        copy = pltpu.make_async_copy(send_ref.at[p, slot], back_hbm.at[p, slot], out_sem.at[2 + p])
        copy.start()
        outs.append(copy)

    pending = [(p, offset) for p in range(PHASES) for offset in ORDER]

    def send_back(count):
        for _ in range(count):
            p, (dz, dy, dc) = pending[len(b_copies)]
            i = dz * 4 + dy * 2 + dc
            slot = pl.ds(2 * i, CAP)
            copy = remote(
                send_ref.at[p, slot], back_hbm.at[p, slot], b_send.at[p, i], b_recv.at[p, i],
                dp_dev((NZ - dz) % NZ, dy, dc),
            )
            copy.start()
            b_copies.append(copy)

    b_sent = []

    def wait_sent(count):
        for _ in range(count):
            b_copies[len(b_sent)].wait_send()
            b_sent.append(1)

    def grad_tile(half, t):
        tile = (z + STEPS[t]) % NZ
        c = pl.ds(pl.multiple_of(half * hq + tile * grad_cols, grad_cols), grad_cols)
        return mm(enc_t_ref[...], dkv_ref[:, :, c].reshape(n_req * BLOCK, grad_cols)).reshape(
            N_FSDP, w_rows, grad_cols
        )

    g_copies, r_copies = [], []

    def for_sibling(t):
        gs_ref[t] = grad_tile(sib, t).astype(bf16)
        copy = remote(gs_ref.at[t], gr_ref.at[t], g_send.at[t], g_recv.at[t], dp_dev(0, 0, 1))
        copy.start()
        g_copies.append(copy)

    def for_owners(t):
        own = grad_tile(core, t)
        g_copies[t].wait()
        gs_ref[t] = (own + gr_ref[t].astype(f32)).astype(bf16)
        for j, (dyh, dx) in enumerate(FS):
            dst_fs = ((yh + dyh) % NYH) * NX + (x + dx) % NX
            copy = remote(gs_ref.at[t, dst_fs], rs_ref.at[t, j], r_send.at[t, j], r_recv.at[t, j], fs_dev(dyh, dx))
            copy.start()
            r_copies.append(copy)

    part_cols = grad_cols // NY
    d_copies = []

    def reduce_tile(t):
        for copy in r_copies[t * len(FS):(t + 1) * len(FS)]:
            copy.wait_recv()
        total = gs_ref[t, fs].astype(f32)
        for j in range(len(FS)):
            total = total + rs_ref[t, j].astype(f32)
        for s in range(NY):
            ds_ref[t, s] = total[:, s * part_cols:(s + 1) * part_cols].astype(bf16)
        for dy in range(NY):
            m = len(d_copies)
            if (STEPS[t], dy) != (0, 0):
                copy = remote(
                    ds_ref.at[t, (yl + dy) % NY], dr_ref.at[m], d_send.at[m], d_recv.at[m], dp_dev(STEPS[t], dy, 0)
                )
                copy.start()
                d_copies.append(copy)

    d_neigh(0)
    send_back(15)
    enc_rows = jnp.concatenate([enc_ref[p] for p in range(PHASES)], axis=1).reshape(n_req * BLOCK, enc_width)
    enc_t_ref[...] = enc_rows.T
    for_sibling(0)
    for_sibling(1)
    for_owners(0)
    for_owners(1)
    d_neigh(1)
    send_back(15)
    for_sibling(2)
    for_sibling(3)
    for_owners(2)
    for_owners(3)
    d_neigh(2)
    d_neigh(3)

    @pl.loop(0, n_req // NEIGH)
    def _(win):
        attend_outputs(win, kv_ref, probs_ref, dsc_ref, q_ref, c_ref)

    for k, (src, dst) in enumerate(((q_ref, att_hbm), (c_ref, dq_hbm))):
        copy = pltpu.make_async_copy(src, dst, out_sem.at[k])
        copy.start()
        outs.append(copy)
    reduce_tile(0)
    wait_sent(15)
    send_back(8)
    reduce_tile(1)
    reduce_tile(2)
    wait_sent(8)
    send_back(7)
    reduce_tile(3)
    send_back(8)

    own_chip = z * NY + yl
    chips = [(dz, dy) for dz in range(NZ) for dy in range(NY) if (dz, dy) != (0, 0)]
    total = ds_ref[STEPS.index(0), yl].astype(f32)
    for m in range(len(chips)):
        d_copies[m].wait_recv()
        total = total + dr_ref[m].astype(f32)
    ag_ref[...] = total.astype(bf16)

    def piece(chip):
        return grad_hbm.at[core * (NZ * NY) + chip]

    copy = pltpu.make_async_copy(ag_ref, piece(own_chip), out_sem.at[2 + PHASES])
    copy.start()
    outs.append(copy)
    o_copies, s_copies = [], []
    for m, (dz, dy) in enumerate(chips):
        copy = remote(ag_ref, piece(own_chip), o_send.at[m], o_recv.at[m], dp_dev(dz, dy, 0))
        copy.start()
        o_copies.append(copy)
    copy = remote(ag_ref, piece(own_chip), s_send.at[len(chips)], s_recv.at[len(chips)], dp_dev(0, 0, 1))
    copy.start()
    s_copies.append(copy)
    send_back(len(pending) - len(b_copies))
    for m, (dz, dy) in enumerate(chips):
        o_copies[m].wait_recv()
        part = piece(((z + NZ - dz) % NZ) * NY + (yl + dy) % NY)
        copy = remote(part, part, s_send.at[m], s_recv.at[m], dp_dev(0, 0, 1))
        copy.start()
        s_copies.append(copy)
    for copy in outs:
        copy.wait()
    for copy in w_copies + ws_copies + r_copies + d_copies + o_copies + b_copies[len(b_sent):]:
        copy.wait_send()
    for copy in b_copies:
        copy.wait_recv()
    for copy in s_copies:
        copy.wait()


def main_call(table, queries, enc_store, weight, cotangent):
    tokens, hq = queries.shape
    blk_dev, _, enc_width = enc_store.shape
    n_req = tokens // WIN * NEIGH
    w_rows = weight.shape[0]
    n_slots = N_DP * CAP
    n_tiles, grad_cols, pairs = NZ, hq // NZ, hq // (2 * HEAD)
    n_chips = NZ * NY
    hbm = pl.BlockSpec(memory_space=pl.ANY)
    vm = pltpu.VMEM
    sem = pltpu.SemaphoreType.DMA
    recv = vm((n_slots, ROWS, enc_width), bf16)
    scratch = [
        vm((tokens, hq), bf16), vm((tokens, hq), bf16), vm(enc_store.shape, bf16),
        vm(weight.shape, bf16), vm((N_FSDP, NC, w_rows // NC, 2 * hq), bf16), vm((PHASES, n_slots, ROWS, enc_width), bf16),
        recv, recv, recv, recv,
        vm((n_req, BLOCK, 2 * hq), bf16), vm((n_req, BLOCK, 2 * hq), bf16),
        vm((n_req // NEIGH, pairs, NEIGH * BLOCK, 2 * WIN), bf16),
        vm((n_req // NEIGH, pairs, NEIGH * BLOCK, 2 * WIN), bf16), vm((PHASES, n_req, ROWS, enc_width), bf16),
        vm((enc_width, n_req * BLOCK), bf16),
        vm((n_req, ROWS, enc_width), bf16),
        vm((n_tiles, N_FSDP, w_rows, grad_cols), bf16),
        vm((n_tiles, N_FSDP, w_rows, grad_cols), bf16), vm((n_tiles, N_FSDP - 1, w_rows, grad_cols), bf16),
        vm((NZ, NY, w_rows, hq // n_chips), bf16), vm((n_chips - 1, w_rows, hq // n_chips), bf16),
        vm((w_rows, hq // n_chips), bf16),
        pltpu.SMEM((n_req,), jnp.int32), pltpu.SMEM((n_slots,), jnp.int32),
        sem((4,)), sem((3 + PHASES,)), sem((PHASES, N_DP)), sem((PHASES, N_DP)),
        sem((N_FSDP - 1,)), sem((N_FSDP - 1,)), sem((N_FSDP - 1,)), sem((N_FSDP - 1,)),
        sem((PHASES, N_DP)), sem((PHASES, N_DP)), sem((n_tiles,)), sem((n_tiles,)),
        sem((n_tiles, N_FSDP - 1)), sem((n_tiles, N_FSDP - 1)), sem((n_chips - 1,)), sem((n_chips - 1,)),
        sem((n_chips - 1,)), sem((n_chips - 1,)), sem((n_chips,)), sem((n_chips,)),
    ]
    return pl.pallas_call(
        main_kernel,
        out_shape=[
            jax.ShapeDtypeStruct((tokens, hq), bf16),
            jax.ShapeDtypeStruct((tokens, hq), bf16),
            jax.ShapeDtypeStruct((PHASES, n_slots, ROWS, enc_width), bf16),
            jax.ShapeDtypeStruct((NC * n_chips, w_rows, hq // n_chips), bf16),
            jax.ShapeDtypeStruct((n_slots,), jnp.int32),
        ],
        in_specs=[pl.BlockSpec(memory_space=pltpu.SMEM), hbm, hbm, hbm, hbm],
        out_specs=[hbm, hbm, hbm, hbm, pl.BlockSpec(memory_space=pltpu.SMEM)],
        scratch_shapes=scratch,
        compiler_params=pltpu.CompilerParams(collective_id=0, has_side_effects=True, vmem_limit_bytes=63 << 20),
        name="attend_exchange",
    )(table, queries, enc_store, weight, cotangent)


def last_kernel(
    scale, pick_ref, back_ref, g_ref, att_in, dq_in, store_ref, grad_ref, att_out, dq_out, acc_ref
):
    att_out[...] = att_in[...]
    dq_out[...] = dq_in[...]
    acc_ref[...] = jnp.zeros_like(acc_ref)
    for i in range(pick_ref.shape[0]):
        @pl.when(pick_ref[i] >= 0)
        def _():
            acc_ref[pick_ref[i]] += back_ref[0, i].astype(f32)

    store_ref[...] = acc_ref[...].astype(bf16)

    @pl.when(pl.program_id(0) == 0)
    def _():
        cols = g_ref.shape[2]
        for half in range(NC):
            for chip in range(NZ * NY):
                grad_ref[:, half, chip * cols:(chip + 1) * cols] = g_ref[half * NZ * NY + chip].astype(f32) * scale


def last_call(picks, back, grads, attended, d_queries, store_shape, w_rows, hq):
    blk_dev, _, enc_width = store_shape
    tokens = attended.shape[0]
    rows = pl.BlockSpec((tokens // PHASES, hq), lambda p: (p, 0))
    scale = float(tokens // WIN * NEIGH * BLOCK * N_DP * N_FSDP) ** (-0.5)
    return pl.pallas_call(
        functools.partial(last_kernel, scale),
        grid=(PHASES,),
        out_shape=[
            jax.ShapeDtypeStruct(store_shape, bf16),
            jax.ShapeDtypeStruct((w_rows, NC, hq), f32),
            jax.ShapeDtypeStruct(attended.shape, bf16),
            jax.ShapeDtypeStruct(d_queries.shape, bf16),
        ],
        in_specs=[
            pl.BlockSpec(memory_space=pltpu.SMEM),
            pl.BlockSpec((1,) + back.shape[1:], lambda p: (p, 0, 0, 0)),
            pl.BlockSpec(grads.shape, lambda p: (0, 0, 0)),
            rows, rows,
        ],
        out_specs=[
            pl.BlockSpec((blk_dev, ROWS, enc_width), lambda p: (0, p, 0)),
            pl.BlockSpec((w_rows, NC, hq), lambda p: (0, 0, 0)),
            rows, rows,
        ],
        scratch_shapes=[pltpu.VMEM((blk_dev, ROWS, enc_width), f32)],
        compiler_params=pltpu.CompilerParams(vmem_limit_bytes=62 << 20),
        name="store_gradient",
    )(picks, back, grads, attended, d_queries)


def shards(queries, enc_store, kv_weight, table, cotangent):
    w_rows, _, hq = kv_weight.shape
    attended, d_queries, back, grads, picks = main_call(table.T, queries, enc_store, kv_weight, cotangent)
    d_store, grad_kv, attended, d_queries = last_call(
        picks, back, grads, attended, d_queries, enc_store.shape, w_rows, hq
    )
    return attended, d_queries, d_store, grad_kv


def solution(mesh):
    in_specs = (
        P(("dp", "fsdp"), None),
        P(("dp", "fsdp"), None, None),
        P("fsdp", None, None),
        P(),
        P(("dp", "fsdp"), None),
    )
    out_specs = (
        P(("dp", "fsdp"), None),
        P(("dp", "fsdp"), None),
        P(("dp", "fsdp"), None, None),
        P("fsdp", None, None),
    )
    return jax.shard_map(shards, mesh=mesh, in_specs=in_specs, out_specs=out_specs, check_vma=False)
```

time: 157 us -> 136 us (0.87)
  Pallas kernels: 146 us -> 135 us
  local copies, waits for them, and re-layouts: 10 us -> 0 us
    unnamed x14 -> x0, local copies, waits for them, and re-layouts: 9.21 us -> none
    pallas_call x1, Pallas kernels: 134 us -> 128 us  [main_call(): pl.pallas_call(main_kernel, out_shape=[jax.ShapeDtypeStruct((tokens, hq),...]
    pallas_call x1, Pallas kernels: 12.7 us -> 7.71 us  [last_call(): pl.pallas_call(functools.partial(last_kernel, scale), grid=(PHASES,), out...]
where the time goes in v2:
time: 136 us
  Pallas kernels  135 us (99%)
    pallas_call x1, Pallas kernels, main_call(): pl.pallas_call(main_kernel, out_shape=[jax.ShapeDtypeStruct((tokens, hq),...  128 us
    pallas_call x1, Pallas kernels, last_call(): pl.pallas_call(functools.partial(last_kernel, scale), grid=(PHASES,), out...  7.71 us

profile of v2, /device:TPU:1, one launch (start us, length us, event | category | flops | bytes accessed | tf_op | source)
XLA Modules:
  0.0 136.2 jit_solution(13377473029627159415)
XLA Ops:
  0.6 127.7 %attend_exchange.1 = (bf16[384,2048]{1,0:T(8,128)(2,1)}, bf16[384,2048]{1,0:T(8,128)(2,1)}, bf16[4,32,32,512]{3,2,1,0:T(8,128)(2,1)}, bf16[16,64,256]{2,1,0:T(8,128)(2,1)}, s32[32]{0:T(128)}) custom-call(s32[2,768]{1,0:T(2,128)} %bitcast.1, bf16[384,2048]{1,0:T(8,128)(2,1)} %q_hbm.1, bf16[16,128,512]{2,1,0:T(8,128)(2,1)} %store_hbm.1, ...), custom_call_target="tpu_custom_call" | custom-call | tf_op jit(solution)/shard_map/attend_exchange/pallas_call | solution.py:479
  128.4 7.7 %store_gradient.1 = (bf16[16,128,512]{2,1,0:T(8,128)(2,1)}, f32[64,2,2048]{2,1,0:T(2,128)}, bf16[384,2048]{1,0:T(8,128)(2,1)}, bf16[384,2048]{1,0:T(8,128)(2,1)}) custom-call(s32[32]{0:T(128)} %get-tuple-element.13.pick_ref, bf16[4,32,32,512]{3,2,1,0:T(8,128)(2,1)} %get-tuple-element.14.back_ref, bf16[16,64,256]{2,1,0:T(8,128)(2,1)} %get-tuple-element.15.g_ref, ...), custom_call_target="tpu_custom_call" | custom-call | tf_op jit(solution)/shard_map/store_gradient/pallas_call | solution.py:522

commit v3 on v2

--- a/solution.py
+++ b/solution.py
@@ -18,6 +18,7 @@
 PHASES = 4
 ROWS = BLOCK // PHASES
 SCALE = HEAD ** (-0.5)
+LOG2E = 1.4426950408889634
 MESH = pl.DeviceIdType.MESH
 f32, bf16 = jnp.float32, jnp.bfloat16
 ORDER = (
@@ -65,7 +66,7 @@
 
 def pair_softmax(first):
     query2, cot2, scores, d_probs = first
-    expo = jnp.exp((scores - jnp.max(scores, axis=0, keepdims=True)) * SCALE)
+    expo = jnp.exp2((scores - jnp.max(scores, axis=0, keepdims=True)) * (SCALE * LOG2E))
     probs = expo * (1.0 / jnp.sum(expo, axis=0, keepdims=True))
     inner = jnp.sum(d_probs * probs, axis=0, keepdims=True)
     d_scores = ((probs * SCALE) * (d_probs - inner)).astype(bf16)
@@ -87,34 +88,38 @@
     return row, blk, cols, width // (2 * HEAD)
 
 
-def attend(win, q_ref, c_ref, kv_ref, dkv_ref, probs_ref, ds_ref):
+def attend(wins, q_ref, c_ref, kv_ref, dkv_ref, probs_ref, ds_ref):
     width = q_ref.shape[1]
-    row, blk, cols, pairs = window_slices(win, width)
     keys_of = NEIGH * BLOCK
-    loaded = [
-        (
-            q_ref[row, cols(i, 0)],
-            c_ref[row, cols(i, 0)],
-            kv_ref[blk, :, cols(i, 0)].reshape(keys_of, 2 * HEAD),
-            kv_ref[blk, :, cols(i, width)].reshape(keys_of, 2 * HEAD),
-        )
-        for i in range(pairs)
-    ]
+    items, loaded = [], []
+    for win in wins:
+        row, blk, cols, pairs = window_slices(win, width)
+        for i in range(pairs):
+            items.append((win, blk, i, cols(i, 0), cols(i, width)))
+            loaded.append(
+                (
+                    q_ref[row, cols(i, 0)],
+                    c_ref[row, cols(i, 0)],
+                    kv_ref[blk, :, cols(i, 0)].reshape(keys_of, 2 * HEAD),
+                    kv_ref[blk, :, cols(i, width)].reshape(keys_of, 2 * HEAD),
+                )
+            )
+    count = len(items)
     ahead = 2
-    first = [pair_first(loaded[i]) for i in range(min(ahead, pairs))]
+    first = [pair_first(loaded[i]) for i in range(ahead)]
     second, last = [], []
-    for i in range(pairs):
+    for i in range(count):
         second.append(pair_softmax(first[i]))
-        if i + ahead < pairs:
+        if i + ahead < count:
             first.append(pair_first(loaded[i + ahead]))
         if i >= 1:
             last.append(pair_last(second[i - 1]))
     last.append(pair_last(second[-1]))
-    for i, (probs_b, d_scores, d_key, d_value) in enumerate(last):
+    for (win, blk, i, key_cols, value_cols), (probs_b, d_scores, d_key, d_value) in zip(items, last):
         probs_ref[win, i] = probs_b
         ds_ref[win, i] = d_scores
-        dkv_ref[blk, :, cols(i, 0)] = d_key.reshape(NEIGH, BLOCK, 2 * HEAD)
-        dkv_ref[blk, :, cols(i, width)] = d_value.reshape(NEIGH, BLOCK, 2 * HEAD)
+        dkv_ref[blk, :, key_cols] = d_key.reshape(NEIGH, BLOCK, 2 * HEAD)
+        dkv_ref[blk, :, value_cols] = d_value.reshape(NEIGH, BLOCK, 2 * HEAD)
 
 
 def attend_outputs(win, kv_ref, probs_ref, ds_ref, att_ref, dq_ref):
@@ -276,9 +281,11 @@
     loads[2].wait()
     loads[3].wait()
 
-    @pl.loop(0, n_req // NEIGH)
-    def _(win):
-        attend(win, q_ref, c_ref, kv_ref, dkv_ref, probs_ref, dsc_ref)
+    together = 3
+
+    @pl.loop(0, n_req // NEIGH // together)
+    def _(step):
+        attend([step * together + k for k in range(together)], q_ref, c_ref, kv_ref, dkv_ref, probs_ref, dsc_ref)
 
     outs = []
     for copy in a_copies:
@@ -494,52 +501,91 @@
 
 
 def last_kernel(
-    scale, pick_ref, back_ref, g_ref, att_in, dq_in, store_ref, grad_ref, att_out, dq_out, acc_ref
+    scale, pick_ref, back_hbm, g_hbm, att_in, dq_in, store_hbm, grad_hbm, att_out, dq_out,
+    back_ref, acc_ref, store_ref, g_ref, grad_ref, att_ref, dq_ref,
+    back_sem, g_sem, in_sem, out_sem,
 ):
-    att_out[...] = att_in[...]
-    dq_out[...] = dq_in[...]
+    n_slots = pick_ref.shape[0]
+    blk_dev, _, rows, width = acc_ref.shape
+    parts = in_sem.shape[1]
+    share = att_ref.shape[0] // parts
+
+    def slot_copy(i):
+        return pltpu.make_async_copy(back_hbm.at[:, i], back_ref.at[i], back_sem.at[i])
+
+    def each_filled(body):
+        def step(i, carry):
+            @pl.when(pick_ref[i] >= 0)
+            def _():
+                body(i)
+            return carry
+
+        lax.fori_loop(0, n_slots, step, 0)
+
+    g_copy = pltpu.make_async_copy(g_hbm, g_ref, g_sem)
+    g_copy.start()
+    each_filled(lambda i: slot_copy(i).start())
+    ins, outs = [], []
+    for part in range(parts):
+        rng = pl.ds(part * share, share)
+        for k, (src, buf, dst) in enumerate(((att_in, att_ref, att_out), (dq_in, dq_ref, dq_out))):
+            copy = pltpu.make_async_copy(src.at[rng], buf.at[rng], in_sem.at[k, part])
+            copy.start()
+            ins.append((copy, pltpu.make_async_copy(buf.at[rng], dst.at[rng], out_sem.at[k, part])))
     acc_ref[...] = jnp.zeros_like(acc_ref)
-    for i in range(pick_ref.shape[0]):
-        @pl.when(pick_ref[i] >= 0)
-        def _():
-            acc_ref[pick_ref[i]] += back_ref[0, i].astype(f32)
-
-    store_ref[...] = acc_ref[...].astype(bf16)
-
-    @pl.when(pl.program_id(0) == 0)
-    def _():
-        cols = g_ref.shape[2]
-        for half in range(NC):
-            for chip in range(NZ * NY):
-                grad_ref[:, half, chip * cols:(chip + 1) * cols] = g_ref[half * NZ * NY + chip].astype(f32) * scale
+    g_copy.wait()
+    cols = g_ref.shape[2]
+    for half in range(NC):
+        for chip in range(NZ * NY):
+            grad_ref[:, half, chip * cols:(chip + 1) * cols] = g_ref[half * NZ * NY + chip].astype(f32) * scale
+    copy = pltpu.make_async_copy(grad_ref, grad_hbm, out_sem.at[2, 0])
+    copy.start()
+    outs.append(copy)
+
+    def add(i):
+        slot_copy(i).wait()
+        acc_ref[pick_ref[i]] += back_ref[i].astype(f32)
+
+    each_filled(add)
+    for copy, out in ins:
+        copy.wait()
+        out.start()
+        outs.append(out)
+    some = blk_dev // parts
+    for part in range(parts):
+        rng = pl.ds(part * some, some)
+        store_ref[rng] = acc_ref[rng].astype(bf16).reshape(some, BLOCK, width)
+        copy = pltpu.make_async_copy(store_ref.at[rng], store_hbm.at[rng], out_sem.at[3, part])
+        copy.start()
+        outs.append(copy)
+    for copy in outs:
+        copy.wait()
 
 
 def last_call(picks, back, grads, attended, d_queries, store_shape, w_rows, hq):
     blk_dev, _, enc_width = store_shape
     tokens = attended.shape[0]
-    rows = pl.BlockSpec((tokens // PHASES, hq), lambda p: (p, 0))
+    n_slots = back.shape[1]
+    parts = 4
+    hbm = pl.BlockSpec(memory_space=pl.ANY)
+    vm, sem = pltpu.VMEM, pltpu.SemaphoreType.DMA
     scale = float(tokens // WIN * NEIGH * BLOCK * N_DP * N_FSDP) ** (-0.5)
     return pl.pallas_call(
         functools.partial(last_kernel, scale),
-        grid=(PHASES,),
         out_shape=[
             jax.ShapeDtypeStruct(store_shape, bf16),
             jax.ShapeDtypeStruct((w_rows, NC, hq), f32),
             jax.ShapeDtypeStruct(attended.shape, bf16),
             jax.ShapeDtypeStruct(d_queries.shape, bf16),
         ],
-        in_specs=[
-            pl.BlockSpec(memory_space=pltpu.SMEM),
-            pl.BlockSpec((1,) + back.shape[1:], lambda p: (p, 0, 0, 0)),
-            pl.BlockSpec(grads.shape, lambda p: (0, 0, 0)),
-            rows, rows,
+        in_specs=[pl.BlockSpec(memory_space=pltpu.SMEM), hbm, hbm, hbm, hbm],
+        out_specs=[hbm, hbm, hbm, hbm],
+        scratch_shapes=[
+            vm((n_slots, PHASES, ROWS, enc_width), bf16), vm((blk_dev, PHASES, ROWS, enc_width), f32),
+            vm(store_shape, bf16), vm(grads.shape, bf16), vm((w_rows, NC, hq), f32),
+            vm(attended.shape, bf16), vm(attended.shape, bf16),
+            sem((n_slots,)), sem(()), sem((2, parts)), sem((4, parts)),
         ],
-        out_specs=[
-            pl.BlockSpec((blk_dev, ROWS, enc_width), lambda p: (0, p, 0)),
-            pl.BlockSpec((w_rows, NC, hq), lambda p: (0, 0, 0)),
-            rows, rows,
-        ],
-        scratch_shapes=[pltpu.VMEM((blk_dev, ROWS, enc_width), f32)],
         compiler_params=pltpu.CompilerParams(vmem_limit_bytes=62 << 20),
         name="store_gradient",
     )(picks, back, grads, attended, d_queries)

time: 136 us -> 133 us (0.978)
  Pallas kernels: 135 us -> 132 us
    pallas_call x1, Pallas kernels: 7.71 us -> 5.88 us  [last_call(): pl.pallas_call(functools.partial(last_kernel, scale), out_shape=[jax.Shap...]
where the time goes in v3:
time: 133 us
  Pallas kernels  132 us (99%)
    pallas_call x1, Pallas kernels, main_call(): pl.pallas_call(main_kernel, out_shape=[jax.ShapeDtypeStruct((tokens, hq),...  126 us
    pallas_call x1, Pallas kernels, last_call(): pl.pallas_call(functools.partial(last_kernel, scale), out_shape=[jax.Shap...  5.88 us

profile of v3, /device:TPU:1, one launch (start us, length us, event | category | flops | bytes accessed | tf_op | source)
XLA Modules:
  0.0 133.1 jit_solution(8722395278906662674)
XLA Ops:
  0.6 126.4 %attend_exchange.1 = (bf16[384,2048]{1,0:T(8,128)(2,1)}, bf16[384,2048]{1,0:T(8,128)(2,1)}, bf16[4,32,32,512]{3,2,1,0:T(8,128)(2,1)}, bf16[16,64,256]{2,1,0:T(8,128)(2,1)}, s32[32]{0:T(128)}) custom-call(s32[2,768]{1,0:T(2,128)} %bitcast.1, bf16[384,2048]{1,0:T(8,128)(2,1)} %q_hbm.1, bf16[16,128,512]{2,1,0:T(8,128)(2,1)} %store_hbm.1, ...), custom_call_target="tpu_custom_call" | custom-call | tf_op jit(solution)/shard_map/attend_exchange/pallas_call | solution.py:486
  127.1 5.9 %store_gradient.1 = (bf16[16,128,512]{2,1,0:T(8,128)(2,1)}, f32[64,2,2048]{2,1,0:T(2,128)}, bf16[384,2048]{1,0:T(8,128)(2,1)}, bf16[384,2048]{1,0:T(8,128)(2,1)}) custom-call(s32[32]{0:T(128)} %get-tuple-element.13.pick_ref, bf16[4,32,32,512]{3,2,1,0:T(8,128)(2,1)} %get-tuple-element.14.back_hbm, bf16[16,64,256]{2,1,0:T(8,128)(2,1)} %get-tuple-element.15.g_hbm, ...), custom_call_target="tpu_custom_call" | custom-call | tf_op jit(solution)/shard_map/store_gradient/pallas_call | solution.py:573

commit v4 on v3

--- a/solution.py
+++ b/solution.py
@@ -15,8 +15,9 @@
 NZ, NY, NC = 4, 2, 2
 NYH, NX = 2, 4
 N_DP, N_FSDP = NZ * NY * NC, NYH * NX
-PHASES = 4
-ROWS = BLOCK // PHASES
+PHASE_ROWS = (48, 32, 32, 16)
+PHASE_START = (0, 48, 80, 112)
+PHASES = len(PHASE_ROWS)
 SCALE = HEAD ** (-0.5)
 LOG2E = 1.4426950408889634
 MESH = pl.DeviceIdType.MESH
@@ -151,13 +152,15 @@
 def main_kernel(
     table_ref, q_hbm, store_hbm, w_hbm, c_hbm,
     att_hbm, dq_hbm, back_hbm, grad_hbm, pick_ref,
-    q_ref, c_ref, store_ref, w_raw, w_ref, send_ref, recv0, recv1, recv2, recv3,
+    q_ref, c_ref, store_ref, w_raw, w_ref,
+    send0, send1, send2, send3, recv0, recv1, recv2, recv3,
     kv_ref, dkv_ref, probs_ref, dsc_ref, enc_ref, enc_t_ref, dn_ref,
     gs_ref, gr_ref, rs_ref, ds_ref, dr_ref, ag_ref,
     slot_ref, inv_ref,
     in_sem, out_sem, a_send, a_recv, w_send, w_recv, ws_send, ws_recv,
     b_send, b_recv, g_send, g_recv, r_send, r_recv, d_send, d_recv, o_send, o_recv, s_send, s_recv,
 ):
+    sends = (send0, send1, send2, send3)
     recvs = (recv0, recv1, recv2, recv3)
     dp, fs, z, yl, core, yh, x = place()
     blk_dev = store_ref.shape[0]
@@ -183,13 +186,19 @@
             src_ref=src, dst_ref=dst, send_sem=ssem, recv_sem=rsem, device_id=dev, device_id_type=MESH
         )
 
+    def rows_of(p):
+        return pl.ds(PHASE_START[p], PHASE_ROWS[p])
+
+    store_loads = [
+        pltpu.make_async_copy(store_hbm.at[:, rows_of(p)], store_ref.at[:, rows_of(p)], in_sem.at[3 + p])
+        for p in range(PHASES)
+    ]
     loads = [
-        pltpu.make_async_copy(store_hbm, store_ref, in_sem.at[0]),
-        pltpu.make_async_copy(w_hbm, w_raw, in_sem.at[1]),
-        pltpu.make_async_copy(q_hbm, q_ref, in_sem.at[2]),
-        pltpu.make_async_copy(c_hbm, c_ref, in_sem.at[3]),
+        pltpu.make_async_copy(w_hbm, w_raw, in_sem.at[0]),
+        pltpu.make_async_copy(q_hbm, q_ref, in_sem.at[1]),
+        pltpu.make_async_copy(c_hbm, c_ref, in_sem.at[2]),
     ]
-    for copy in loads:
+    for copy in store_loads + loads:
         copy.start()
     barrier = pltpu.get_barrier_semaphore()
     partners = [dp_dev(*o) for o in ORDER] + [fs_dev(*o) for o in FS]
@@ -204,24 +213,25 @@
         return carry
 
     lax.fori_loop(0, N_DP, picks, 0)
-    loads[0].wait()
+    for copy in store_loads:
+        copy.wait()
     pl.semaphore_wait(barrier, len(partners))
 
     a_copies, w_copies = [], []
     for p in range(PHASES):
-        rows = pl.ds(p * ROWS, ROWS)
+        rows = rows_of(p)
         for dz, dy, dc in ORDER:
             i = dz * 4 + dy * 2 + dc
             for k in range(CAP):
-                send_ref[p, 2 * i + k] = store_ref[jnp.maximum(pick_ref[2 * i + k], 0), rows, :]
+                sends[p][2 * i + k] = store_ref[jnp.maximum(pick_ref[2 * i + k], 0), rows, :]
             slot = pl.ds(2 * i, CAP)
-            copy = remote(send_ref.at[p, slot], recvs[p].at[slot], a_send.at[p, i], a_recv.at[p, i], dp_dev(dz, dy, dc))
+            copy = remote(sends[p].at[slot], recvs[p].at[slot], a_send.at[p, i], a_recv.at[p, i], dp_dev(dz, dy, dc))
             copy.start()
             a_copies.append(copy)
         for k in range(CAP):
             recvs[p][k] = store_ref[jnp.maximum(pick_ref[k], 0), rows, :]
         if p == 0:
-            loads[1].wait()
+            loads[0].wait()
             for part in range(NC):
                 for kind in range(2):
                     w_ref[fs, part, :, kind * hq:(kind + 1) * hq] = w_raw[part * w_half:(part + 1) * w_half, kind, :]
@@ -268,18 +278,20 @@
     for p in range(PHASES):
         for copy in a_copies[p * len(ORDER):(p + 1) * len(ORDER)]:
             copy.wait_recv()
-        rows = pl.ds(p * ROWS, ROWS)
+        rows = rows_of(p)
         for r in range(n_req):
-            enc_ref[p, r] = recvs[p][slot_ref[r]]
+            enc_ref[r, rows, :] = recvs[p][slot_ref[r]]
+        some = PHASE_ROWS[p]
 
         @pl.loop(0, kv_ref.shape[2] // 1024)
         def _(t):
             c = pl.ds(pl.multiple_of(t * 1024, 1024), 1024)
-            out = mm(enc_ref[p].reshape(n_req * ROWS, enc_width), w_ref[:, :, :, c].reshape(enc_width, 1024))
-            kv_ref[:, rows, c] = out.astype(bf16).reshape(n_req, ROWS, 1024)
-
+            lhs = enc_ref[:, rows, :].reshape(n_req * some, enc_width)
+            out = mm(lhs, w_ref[:, :, :, c].reshape(enc_width, 1024))
+            kv_ref[:, rows, c] = out.astype(bf16).reshape(n_req, some, 1024)
+
+    loads[1].wait()
     loads[2].wait()
-    loads[3].wait()
 
     together = 3
 
@@ -294,24 +306,24 @@
     b_copies = []
 
     def d_neigh(p):
-        rows = pl.ds(p * ROWS, ROWS)
-        lhs = dkv_ref[:, rows, :].reshape(n_req * ROWS, 2 * hq)
+        rows, some = rows_of(p), PHASE_ROWS[p]
+        lhs = dkv_ref[:, rows, :].reshape(n_req * some, 2 * hq)
 
         @pl.loop(0, 2)
         def _(t):
             part = w_ref[pl.ds(t * (N_FSDP // 2), N_FSDP // 2)].reshape(enc_width // 2, 2 * hq)
             c = pl.ds(pl.multiple_of(t * (enc_width // 2), enc_width // 2), enc_width // 2)
-            dn_ref[:, :, c] = mm_nt(lhs, part).astype(bf16).reshape(n_req, ROWS, enc_width // 2)
+            dn_ref[:, :some, c] = mm_nt(lhs, part).astype(bf16).reshape(n_req, some, enc_width // 2)
 
         for i in range(N_DP):
             for k in range(CAP):
-                send_ref[p, 2 * i + k] = dn_ref[inv_ref[2 * i + k]]
+                sends[p][2 * i + k] = dn_ref[inv_ref[2 * i + k], :some, :]
         slot = pl.ds(0, CAP)
-        copy = pltpu.make_async_copy(send_ref.at[p, slot], back_hbm.at[p, slot], out_sem.at[2 + p])
+        copy = pltpu.make_async_copy(sends[p].at[slot], back_hbm.at[slot, rows], out_sem.at[2 + p])
         copy.start()
         outs.append(copy)
 
-    pending = [(p, offset) for p in range(PHASES) for offset in ORDER]
+    pending = [(p, offset) for p in reversed(range(PHASES)) for offset in ORDER]
 
     def send_back(count):
         for _ in range(count):
@@ -319,7 +331,7 @@
             i = dz * 4 + dy * 2 + dc
             slot = pl.ds(2 * i, CAP)
             copy = remote(
-                send_ref.at[p, slot], back_hbm.at[p, slot], b_send.at[p, i], b_recv.at[p, i],
+                sends[p].at[slot], back_hbm.at[slot, rows_of(p)], b_send.at[p, i], b_recv.at[p, i],
                 dp_dev((NZ - dz) % NZ, dy, dc),
             )
             copy.start()
@@ -377,22 +389,23 @@
                 copy.start()
                 d_copies.append(copy)
 
-    d_neigh(0)
+    d_neigh(3)
     send_back(15)
-    enc_rows = jnp.concatenate([enc_ref[p] for p in range(PHASES)], axis=1).reshape(n_req * BLOCK, enc_width)
-    enc_t_ref[...] = enc_rows.T
+    d_neigh(2)
+    send_back(15)
+    enc_t_ref[...] = enc_ref[...].reshape(n_req * BLOCK, enc_width).T
     for_sibling(0)
     for_sibling(1)
     for_owners(0)
     for_owners(1)
-    d_neigh(1)
-    send_back(15)
     for_sibling(2)
     for_sibling(3)
     for_owners(2)
     for_owners(3)
-    d_neigh(2)
-    d_neigh(3)
+    d_neigh(1)
+    wait_sent(15)
+    send_back(8)
+    d_neigh(0)
 
     @pl.loop(0, n_req // NEIGH)
     def _(win):
@@ -403,12 +416,10 @@
         copy.start()
         outs.append(copy)
     reduce_tile(0)
+    reduce_tile(1)
     wait_sent(15)
-    send_back(8)
-    reduce_tile(1)
+    send_back(7)
     reduce_tile(2)
-    wait_sent(8)
-    send_back(7)
     reduce_tile(3)
     send_back(8)
 
@@ -462,22 +473,22 @@
     hbm = pl.BlockSpec(memory_space=pl.ANY)
     vm = pltpu.VMEM
     sem = pltpu.SemaphoreType.DMA
-    recv = vm((n_slots, ROWS, enc_width), bf16)
+    slot_refs = [vm((n_slots, rows, enc_width), bf16) for rows in PHASE_ROWS]
     scratch = [
         vm((tokens, hq), bf16), vm((tokens, hq), bf16), vm(enc_store.shape, bf16),
-        vm(weight.shape, bf16), vm((N_FSDP, NC, w_rows // NC, 2 * hq), bf16), vm((PHASES, n_slots, ROWS, enc_width), bf16),
-        recv, recv, recv, recv,
+        vm(weight.shape, bf16), vm((N_FSDP, NC, w_rows // NC, 2 * hq), bf16),
+        *slot_refs, *slot_refs,
         vm((n_req, BLOCK, 2 * hq), bf16), vm((n_req, BLOCK, 2 * hq), bf16),
         vm((n_req // NEIGH, pairs, NEIGH * BLOCK, 2 * WIN), bf16),
-        vm((n_req // NEIGH, pairs, NEIGH * BLOCK, 2 * WIN), bf16), vm((PHASES, n_req, ROWS, enc_width), bf16),
+        vm((n_req // NEIGH, pairs, NEIGH * BLOCK, 2 * WIN), bf16), vm((n_req, BLOCK, enc_width), bf16),
         vm((enc_width, n_req * BLOCK), bf16),
-        vm((n_req, ROWS, enc_width), bf16),
+        vm((n_req, max(PHASE_ROWS), enc_width), bf16),
         vm((n_tiles, N_FSDP, w_rows, grad_cols), bf16),
         vm((n_tiles, N_FSDP, w_rows, grad_cols), bf16), vm((n_tiles, N_FSDP - 1, w_rows, grad_cols), bf16),
         vm((NZ, NY, w_rows, hq // n_chips), bf16), vm((n_chips - 1, w_rows, hq // n_chips), bf16),
         vm((w_rows, hq // n_chips), bf16),
         pltpu.SMEM((n_req,), jnp.int32), pltpu.SMEM((n_slots,), jnp.int32),
-        sem((4,)), sem((3 + PHASES,)), sem((PHASES, N_DP)), sem((PHASES, N_DP)),
+        sem((3 + PHASES,)), sem((3 + PHASES,)), sem((PHASES, N_DP)), sem((PHASES, N_DP)),
         sem((N_FSDP - 1,)), sem((N_FSDP - 1,)), sem((N_FSDP - 1,)), sem((N_FSDP - 1,)),
         sem((PHASES, N_DP)), sem((PHASES, N_DP)), sem((n_tiles,)), sem((n_tiles,)),
         sem((n_tiles, N_FSDP - 1)), sem((n_tiles, N_FSDP - 1)), sem((n_chips - 1,)), sem((n_chips - 1,)),
@@ -488,7 +499,7 @@
         out_shape=[
             jax.ShapeDtypeStruct((tokens, hq), bf16),
             jax.ShapeDtypeStruct((tokens, hq), bf16),
-            jax.ShapeDtypeStruct((PHASES, n_slots, ROWS, enc_width), bf16),
+            jax.ShapeDtypeStruct((n_slots, BLOCK, enc_width), bf16),
             jax.ShapeDtypeStruct((NC * n_chips, w_rows, hq // n_chips), bf16),
             jax.ShapeDtypeStruct((n_slots,), jnp.int32),
         ],
@@ -506,12 +517,12 @@
     back_sem, g_sem, in_sem, out_sem,
 ):
     n_slots = pick_ref.shape[0]
-    blk_dev, _, rows, width = acc_ref.shape
+    blk_dev = acc_ref.shape[0]
     parts = in_sem.shape[1]
     share = att_ref.shape[0] // parts
 
     def slot_copy(i):
-        return pltpu.make_async_copy(back_hbm.at[:, i], back_ref.at[i], back_sem.at[i])
+        return pltpu.make_async_copy(back_hbm.at[i], back_ref.at[i], back_sem.at[i])
 
     def each_filled(body):
         def step(i, carry):
@@ -554,7 +565,7 @@
     some = blk_dev // parts
     for part in range(parts):
         rng = pl.ds(part * some, some)
-        store_ref[rng] = acc_ref[rng].astype(bf16).reshape(some, BLOCK, width)
+        store_ref[rng] = acc_ref[rng].astype(bf16)
         copy = pltpu.make_async_copy(store_ref.at[rng], store_hbm.at[rng], out_sem.at[3, part])
         copy.start()
         outs.append(copy)
@@ -563,9 +574,7 @@
 
 
 def last_call(picks, back, grads, attended, d_queries, store_shape, w_rows, hq):
-    blk_dev, _, enc_width = store_shape
     tokens = attended.shape[0]
-    n_slots = back.shape[1]
     parts = 4
     hbm = pl.BlockSpec(memory_space=pl.ANY)
     vm, sem = pltpu.VMEM, pltpu.SemaphoreType.DMA
@@ -581,10 +590,10 @@
         in_specs=[pl.BlockSpec(memory_space=pltpu.SMEM), hbm, hbm, hbm, hbm],
         out_specs=[hbm, hbm, hbm, hbm],
         scratch_shapes=[
-            vm((n_slots, PHASES, ROWS, enc_width), bf16), vm((blk_dev, PHASES, ROWS, enc_width), f32),
+            vm(back.shape, bf16), vm(store_shape, f32),
             vm(store_shape, bf16), vm(grads.shape, bf16), vm((w_rows, NC, hq), f32),
             vm(attended.shape, bf16), vm(attended.shape, bf16),
-            sem((n_slots,)), sem(()), sem((2, parts)), sem((4, parts)),
+            sem((back.shape[0],)), sem(()), sem((2, parts)), sem((4, parts)),
         ],
         compiler_params=pltpu.CompilerParams(vmem_limit_bytes=62 << 20),
         name="store_gradient",

time: 133 us -> 132 us (level)
  no operation moved by 1% of the time
where the time goes in v4:
time: 132 us
  Pallas kernels  131 us (99%)
    pallas_call x1, Pallas kernels, main_call(): pl.pallas_call(main_kernel, out_shape=[jax.ShapeDtypeStruct((tokens, hq),...  126 us
    pallas_call x1, Pallas kernels, last_call(): pl.pallas_call(functools.partial(last_kernel, scale), out_shape=[jax.Shap...  5.78 us

profile of v4, /device:TPU:1, one launch (start us, length us, event | category | flops | bytes accessed | tf_op | source)
XLA Modules:
  0.0 132.3 jit_solution(6276688583983253073)
XLA Ops:
  0.6 125.7 %attend_exchange.1 = (bf16[384,2048]{1,0:T(8,128)(2,1)}, bf16[384,2048]{1,0:T(8,128)(2,1)}, bf16[32,128,512]{2,1,0:T(8,128)(2,1)}, bf16[16,64,256]{2,1,0:T(8,128)(2,1)}, s32[32]{0:T(128)}) custom-call(s32[2,768]{1,0:T(2,128)} %bitcast.1, bf16[384,2048]{1,0:T(8,128)(2,1)} %q_hbm.1, bf16[16,128,512]{2,1,0:T(8,128)(2,1)} %store_hbm.1, ...), custom_call_target="tpu_custom_call" | custom-call | tf_op jit(solution)/shard_map/attend_exchange/pallas_call | solution.py:497
  126.3 5.8 %store_gradient.1 = (bf16[16,128,512]{2,1,0:T(8,128)(2,1)}, f32[64,2,2048]{2,1,0:T(2,128)}, bf16[384,2048]{1,0:T(8,128)(2,1)}, bf16[384,2048]{1,0:T(8,128)(2,1)}) custom-call(s32[32]{0:T(128)} %get-tuple-element.13.pick_ref, bf16[32,128,512]{2,1,0:T(8,128)(2,1)} %get-tuple-element.14.back_hbm, bf16[16,64,256]{2,1,0:T(8,128)(2,1)} %get-tuple-element.15.g_hbm, ...), custom_call_target="tpu_custom_call" | custom-call | tf_op jit(solution)/shard_map/store_gradient/pallas_call | solution.py:582
